TPU v7x, 32 devices: a whole 2x2x4 slice. The times are simulated.
32 devices in a mesh: dp: 16 (over z, x, core), tensor: 2 (over y).
Axes of the slice: x: 2, y: 2, z: 4, core: 2. Of those that a mesh axis runs over, the one named last changes fastest.
Arguments:
- tokens: bfloat16 [8192, 2048], P('dp'), may hold values from -6 to 6
- seg_ids: int32 [32, 256], P('dp'), may hold values from 0 to 3, as said below
- q_weight: bfloat16 [2048, 2048], P('dp', 'tensor'), may hold values from -0.125 to 0.125
- k_weight: bfloat16 [2048, 256], P('dp', 'tensor'), may hold values from -0.125 to 0.125
- v_weight: bfloat16 [2048, 256], P('dp', 'tensor'), may hold values from -0.125 to 0.125
- o_weight: bfloat16 [2048, 2048], P('tensor', 'dp'), may hold values from -0.5 to 0.5
- attn_gain: bfloat16 [2048], P('dp'), may hold values from 0.5 to 1.5
- gate_weight: bfloat16 [2048, 5632], P('dp', 'tensor'), may hold values from -0.125 to 0.125
- up_weight: bfloat16 [2048, 5632], P('dp', 'tensor'), may hold values from -0.125 to 0.125
- down_weight: bfloat16 [5632, 2048], P('tensor', 'dp'), may hold values from -0.078125 to 0.078125
- mlp_gain: bfloat16 [2048], P('dp'), may hold values from 0.5 to 1.5
- out_grad: bfloat16 [8192, 2048], P('dp'), may hold values from -6 to 6
Outputs:
- out: bfloat16 [8192, 2048], P('dp')
- in_grad: bfloat16 [8192, 2048], P('dp')
- grad_q_weight: float32 [2048, 2048], P('dp', 'tensor')
- grad_k_weight: float32 [2048, 256], P('dp', 'tensor')
- grad_v_weight: float32 [2048, 256], P('dp', 'tensor')
- grad_o_weight: float32 [2048, 2048], P('tensor', 'dp')
- grad_attn_gain: float32 [2048], P('dp')
- grad_gate_weight: float32 [2048, 5632], P('dp', 'tensor')
- grad_up_weight: float32 [2048, 5632], P('dp', 'tensor')
- grad_down_weight: float32 [5632, 2048], P('tensor', 'dp')
- grad_mlp_gain: float32 [2048], P('dp')
Inputs may be any that keep to these rules, and one draw needn't show every extreme that they name: `seg_ids`: along each row segment numbers never fall; a sequence is the tokens of one number in one row. Row 0 holds a single sequence of 256 tokens.
All inputs are finite; a program needn't handle non-finite values.
Results may differ from a plain program's by a relative error of at most 0.014.
Values may be sent and summed in bfloat16 or wider, within the bound.
A program may use at most 152 MiB of HBM per device.

v0:
```python
import functools

import jax
import jax.numpy as jnp
from jax import lax
from jax.experimental import pallas as pl
from jax.experimental.pallas import tpu as pltpu
from jax.sharding import PartitionSpec as P

HEAD_DIM = 64
norm_eps = 1e-05
MESH = pl.DeviceIdType.MESH
ANY = pl.BlockSpec(memory_space=pl.ANY)
VMEM = pl.BlockSpec(memory_space=pltpu.VMEM)
DMA = pltpu.SemaphoreType.DMA
F32 = jnp.float32
BF16 = jnp.bfloat16


def place():
    d = lax.axis_index("dp")
    t = lax.axis_index("tensor")
    return d, t, d // 4, lax.rem(d // 2, 2), lax.rem(d, 2)


def enter(zn, here):
    d, t, z, x, c = here
    bar = pltpu.get_barrier_semaphore()

    def hail(device):
        pl.semaphore_signal(bar, inc=1, device_id=device, device_id_type=MESH)

    hail((d + 1 - 2 * c, t))
    hail((d + 2 - 4 * x, t))
    hail((d, 1 - t))

    @pl.when(z > 0)
    def _():
        hail((d - 4, t))

    @pl.when(z < zn - 1)
    def _():
        hail((d + 4, t))

    pl.semaphore_wait(bar, 5 - (z == 0).astype(jnp.int32) - (z == zn - 1).astype(jnp.int32))


def farthest_first(zn, z, i):
    up = 1 - (2 * z) // zn
    longer = up * (zn - 1 - z) + (1 - up) * z
    shorter = zn - 1 - longer
    rest = i - (longer - shorter)
    return jnp.where(
        rest < 0,
        z + (2 * up - 1) * (longer - i),
        z + (1 - 2 * lax.rem(jnp.maximum(rest, 0), 2)) * (shorter - jnp.maximum(rest, 0) // 2),
    )


def loop(count, body):
    def step(i, carry):
        body(i)
        return carry

    lax.fori_loop(0, count, step, 0)


def remote(src, dst, send, recv, device):
    return pltpu.make_async_remote_copy(
        src_ref=src, dst_ref=dst, send_sem=send, recv_sem=recv, device_id=device, device_id_type=MESH
    )


def by_rows(count, body, block=16):
    def step(i, carry):
        body(pl.ds(pl.multiple_of(i * block, block), block))
        return carry

    lax.fori_loop(0, count // block, step, 0)


def gather_sems(n, sources, zn):
    return [
        DMA((sources,)),
        DMA((sources,)),
        DMA((sources,)),
        DMA((n, zn)),
        DMA((n, zn)),
        DMA((n,)),
        DMA((n,)),
        DMA((n, 2, zn)),
        DMA((n, zn)),
        DMA((n, 2, zn)),
        DMA((n, zn)),
    ]


def part(ref, core, paired):
    if paired:
        return ref.at[core]
    columns = ref.shape[1] // 2
    return ref.at[:, pl.ds(pl.multiple_of(core * columns, columns), columns)]


class Gather:
    def __init__(self, zn, here, arrays, sems):
        self.zn, self.here = zn, here
        self.full = [full for _, full, _ in arrays]
        self.early = [early for _, _, early in arrays]
        self.sources = [
            (j, i) + source for j, (sources, _, _) in enumerate(arrays) for i, source in enumerate(sources)
        ]
        (
            self.loc,
            self.cs,
            self.cr,
            self.xs,
            self.xr,
            self.es,
            self.er,
            self.zs,
            self.zr,
            self.bs,
            self.br,
        ) = sems

    def unit(self, j, unit, first, count):
        rows = self.full[j].shape[0] // (2 * self.zn)
        return pl.ds(pl.multiple_of(unit * rows + first, 8), count)

    def rows(self, j, unit, early):
        rows = self.full[j].shape[0] // (2 * self.zn)
        late = rows - self.early[j]
        first, count = {None: (0, rows), True: (late, rows - late), False: (0, late)}[early]
        return self.full[j].at[self.unit(j, unit, first, count)]

    def mine(self, s):
        d, t, z, x, c = self.here
        j, _, shard, paired, first, columns = self.sources[s]
        rows = self.full[j].shape[0] // (4 * self.zn)
        return self.full[j].at[self.unit(j, z * 2 + x, c * rows, rows), pl.ds(first, columns)]

    def keep(self, s):
        _, _, shard, paired, _, _ = self.sources[s]
        return pltpu.make_async_copy(part(shard, self.here[4], paired), self.mine(s), self.loc.at[s])

    def give(self, s):
        d, t, z, x, c = self.here
        _, _, shard, paired, _, _ = self.sources[s]
        return remote(
            part(shard, 1 - c, paired), self.mine(s), self.cs.at[s], self.cr.at[s], (d + 1 - 2 * c, t)
        )

    def x_late(self, j, o):
        d, t, z, x, c = self.here
        ref = self.rows(j, o * 2 + x, False)
        return remote(ref, ref, self.xs.at[j, o], self.xr.at[j, o], (d + 2 - 4 * x, t))

    def x_early(self, j):
        d, t, z, x, c = self.here
        ref = self.rows(j, z * 2 + x, True)
        return remote(ref, ref, self.es.at[j], self.er.at[j], (d + 2 - 4 * x, t))

    def along(self, j, o, down):
        d, t, z, x, c = self.here
        ref = self.rows(j, o * 2 + x, None)
        return remote(ref, ref, self.zs.at[j, down, o], self.zr.at[j, o], (d + 4 - 8 * down, t))

    def along_early(self, j, o, down):
        d, t, z, x, c = self.here
        ref = self.rows(j, o * 2 + 1 - x, True)
        return remote(ref, ref, self.bs.at[j, down, o], self.br.at[j, o], (d + 4 - 8 * down, t))

    def start(self):
        for s in range(len(self.sources)):
            self.give(s).start()
            self.keep(s).start()

    def ready(self, arrays):
        for j in arrays:
            for s, source in enumerate(self.sources):
                if source[0] == j:
                    self.keep(s).wait()
                    self.give(s).wait_recv()
            if self.early[j]:
                self.x_early(j).start()

    def start_own(self, arrays):
        z, zn = self.here[2], self.zn
        for j in arrays:
            self.x_late(j, z).start()

            @pl.when(z < zn - 1)
            def _():
                self.along(j, z, 0).start()

            @pl.when(z > 0)
            def _():
                self.along(j, z, 1).start()

    def start_early(self, arrays):
        z, zn = self.here[2], self.zn
        for j in arrays:
            if self.early[j]:
                self.x_early(j).wait_recv()

                @pl.when(z < zn - 1)
                def _():
                    self.along_early(j, z, 0).start()

                @pl.when(z > 0)
                def _():
                    self.along_early(j, z, 1).start()

    def relay(self, k, arrays):
        z, zn = self.here[2], self.zn
        o = farthest_first(zn, z, zn - 1 - k)
        down = (o > z).astype(jnp.int32)
        more = ((o < z) & (z < zn - 1)) | ((o > z) & (z > 0))
        for j in arrays:
            self.along(j, o, down).wait_recv()

            @pl.when(more)
            def _():
                self.along(j, o, down).start()

            self.x_late(j, o).start()
            if self.early[j]:
                self.along_early(j, o, down).wait_recv()

                @pl.when(more)
                def _():
                    self.along_early(j, o, down).start()

    def relays(self, first, arrays):
        loop(max(self.zn - first, 0), lambda i: self.relay(first + i, arrays))

    def arrived(self, j):
        loop(self.zn, lambda o: self.x_late(j, o).wait_recv())

    def finish(self):
        z, zn = self.here[2], self.zn
        for s in range(len(self.sources)):
            self.give(s).wait_send()
        for j in range(len(self.full)):
            if self.early[j]:
                self.x_early(j).wait_send()

            def step(o, j=j):
                self.x_late(j, o).wait_send()

                def sent(down):
                    self.along(j, o, down).wait_send()
                    if self.early[j]:
                        self.along_early(j, o, down).wait_send()

                @pl.when((o <= z) & (z < zn - 1))
                def _():
                    sent(0)

                @pl.when((o >= z) & (z > 0))
                def _():
                    sent(1)

            loop(zn, step)


def scatter_sems(n, outs, zn):
    return [
        DMA((n, zn)),
        DMA((n, zn)),
        DMA((n, zn)),
        DMA((n, zn)),
        DMA((n, zn)),
        DMA((n, zn + 1)),
        DMA((n, 2, zn)),
        DMA((n, zn)),
        DMA((n, zn + 1)),
        DMA((n,)),
        DMA((n,)),
        DMA((outs,)),
        DMA((outs,)),
        DMA((outs,)),
    ]


def scatter_buffers(shapes, early, zn):
    out = []
    for rows, columns in shapes:
        late = rows - early
        out += [
            pltpu.VMEM((zn, late, columns), BF16),
            pltpu.VMEM((zn, late, columns), BF16),
            pltpu.VMEM((zn + 1, late, columns), BF16),
            pltpu.VMEM((zn, 2, early, columns), BF16),
            pltpu.VMEM((zn + 1, 2, early, columns), BF16),
            pltpu.VMEM((early, columns), BF16),
            pltpu.VMEM((rows, columns), F32),
        ]
    return out


SCATTER_BUFFERS = 7


class Scatter:
    def __init__(self, zn, here, early, arrays, sems):
        self.zn, self.here, self.early = zn, here, early
        self.term = [term for term, _, _ in arrays]
        self.buffers = [buffers for _, buffers, _ in arrays]
        self.results = [(j,) + result for j, (_, _, results) in enumerate(arrays) for result in results]
        (
            self.st,
            self.ls,
            self.xs,
            self.xr,
            self.zs,
            self.zr,
            self.bls,
            self.bs,
            self.br,
            self.es,
            self.er,
            self.cs,
            self.cr,
            self.loc,
        ) = sems

    def unit(self, j, o, x, first, count):
        rows = self.term[j].shape[1] // 2
        return self.term[j].at[o, pl.ds(pl.multiple_of(x * rows + first, 16), count)]

    def late(self, j):
        return self.buffers[j][0].shape[1]

    def load(self, j, o):
        return pltpu.make_async_copy(
            self.unit(j, o, self.here[3], 0, self.late(j)), self.buffers[j][0].at[o], self.ls.at[j, o]
        )

    def load_early(self, j, o, other):
        x = self.here[3]
        return pltpu.make_async_copy(
            self.unit(j, o, 1 - x if other else x, self.late(j), self.early),
            self.buffers[j][3].at[o, other],
            self.bls.at[j, other, o],
        )

    def across(self, j, o):
        d, t, z, x, c = self.here
        return remote(
            self.unit(j, o, 1 - x, 0, self.late(j)),
            self.buffers[j][1].at[o],
            self.xs.at[j, o],
            self.xr.at[j, o],
            (d + 2 - 4 * x, t),
        )

    def across_early(self, j):
        d, t, z, x, c = self.here
        return remote(
            self.buffers[j][3].at[z, 1], self.buffers[j][5], self.es.at[j], self.er.at[j], (d + 2 - 4 * x, t)
        )

    def along(self, j, o, slot, down):
        d, t, z, x, c = self.here
        own, line = self.buffers[j][0], self.buffers[j][2]
        return remote(own.at[o], line.at[slot], self.zs.at[j, o], self.zr.at[j, slot], (d + 4 - 8 * down, t))

    def along_early(self, j, o, slot, down):
        d, t, z, x, c = self.here
        own, line = self.buffers[j][3], self.buffers[j][4]
        return remote(own.at[o], line.at[slot], self.bs.at[j, o], self.br.at[j, slot], (d + 4 - 8 * down, t))

    def give(self, r):
        d, t, z, x, c = self.here
        j, out, paired, first, columns = self.results[r]
        rows = out.shape[-2]
        ref = self.buffers[j][6].at[
            pl.ds(pl.multiple_of((1 - c) * rows, rows), rows), pl.ds(first, columns)
        ]
        return remote(ref, part(out, c, paired), self.cs.at[r], self.cr.at[r], (d + 1 - 2 * c, t))

    def keep(self, r):
        c = self.here[4]
        j, out, paired, first, columns = self.results[r]
        rows = out.shape[-2]
        ref = self.buffers[j][6].at[pl.ds(pl.multiple_of(c * rows, rows), rows), pl.ds(first, columns)]
        return pltpu.make_async_copy(ref, part(out, c, paired), self.loc.at[r])

    def store(self, j, o, stage, slot):
        columns = self.term[j].shape[2]
        return pltpu.make_async_copy(
            stage.at[slot, :, pl.ds(0, columns)], self.term[j].at[o], self.st.at[j, o]
        )

    def make(self, j, left, right, stage, between=None):
        z, zn = self.here[2], self.zn
        wide, columns = self.term[j].shape[1:]
        block = min(256, wide)

        def send(i):
            o = farthest_first(zn, z, i)
            self.store(j, o, stage, lax.rem(i, 2)).wait()
            self.across(j, o).start()
            for other in range(2):
                self.load_early(j, o, other).start()
            self.load(j, o).start()

        def compute(i):
            o = farthest_first(zn, z, i)
            slot = lax.rem(i, 2)

            def body(m):
                at = pl.multiple_of(o * wide + m * block, block)
                value = inner_rows(left[:, pl.ds(at, block)], right[...])
                stage[slot, pl.ds(pl.multiple_of(m * block, block), block), pl.ds(0, columns)] = value.astype(
                    BF16
                )

            loop(wide // block, body)
            self.store(j, o, stage, slot).start()

        def both(i):
            compute(i)
            send(i - 1)
            self.hop_early(j, i - 1)

        compute(0)
        if between is not None:
            between()
        loop(zn - 1, lambda i: both(i + 1))
        send(zn - 1)

    def add(self, j, o, slots):
        own, got, line = self.buffers[j][:3]

        def body(at):
            value = own[o, at].astype(F32) + got[o, at].astype(F32)
            for slot in slots:
                value = value + line[slot, at].astype(F32)
            own[o, at] = value.astype(BF16)

        by_rows(own.shape[1], body)

    def add_early(self, j, o, slots):
        own, line = self.buffers[j][3:5]
        for other in range(2):

            def body(at):
                value = own[o, other, at].astype(F32)
                for slot in slots:
                    value = value + line[slot, other, at].astype(F32)
                own[o, other, at] = value.astype(BF16)

            by_rows(own.shape[2], body)

    def route(self, i):
        z, zn = self.here[2], self.zn
        o = farthest_first(zn, z, i)
        down = (o < z).astype(jnp.int32)
        distance = jnp.maximum((o - z) * (1 - 2 * down), 1)
        slot = o + (zn - o) * down * (1 // distance)
        inner = ((o > z) & (z > 0)) | ((o < z) & (z < zn - 1))
        return o, slot, down, inner

    def hop_early(self, j, i):
        o, slot, down, inner = self.route(i)
        for other in range(2):
            self.load_early(j, o, other).wait()

        @pl.when(inner)
        def _():
            self.along_early(j, o, o, down).wait_recv()
            self.add_early(j, o, [o])

        self.along_early(j, o, slot, down).start()

    def hop(self, j, i):
        o, slot, down, inner = self.route(i)
        self.load(j, o).wait()
        self.across(j, o).wait_recv()

        @pl.when(inner)
        def _():
            self.along(j, o, o, down).wait_recv()
            self.add(j, o, [o])

        @pl.when(jnp.logical_not(inner))
        def _():
            self.add(j, o, [])

        self.along(j, o, slot, down).start()

    def late_hops(self, j):
        self.early_home(j)
        loop(self.zn - 1, lambda i: self.hop(j, i))

    def share_of_hops(self, j, i, shares):
        hops = self.zn - 1
        first = i * hops // (shares - 1)
        last = jnp.minimum((i + 1) * hops // (shares - 1), hops)

        def step(hop, carry):
            self.hop(j, hop)
            return carry

        lax.fori_loop(first, last, step, 0)

    def at_home(self, action):
        z, zn = self.here[2], self.zn

        @pl.when((z > 0) & (z < zn - 1))
        def _():
            action([z, zn])

        @pl.when(z == 0)
        def _():
            action([zn])

        @pl.when(z == zn - 1)
        def _():
            action([z])

    def early_home(self, j):
        z = self.here[2]
        for other in range(2):
            self.load_early(j, z, other).wait()

        def home(slots):
            for slot in slots:
                self.along_early(j, z, slot, 0).wait_recv()
            self.add_early(j, z, slots)

        self.at_home(home)
        self.across_early(j).start()

    def finish(self):
        z, zn = self.here[2], self.zn
        n = len(self.term)
        for j in range(n):
            own, got, line, early, _, other_early, total = self.buffers[j]
            late = self.late(j)
            self.load(j, z).wait()
            self.across(j, z).wait_recv()

            def home(slots):
                for slot in slots:
                    self.along(j, z, slot, 0).wait_recv()

                def body(at):
                    value = own[z, at].astype(F32) + got[z, at].astype(F32)
                    for slot in slots:
                        value = value + line[slot, at].astype(F32)
                    total[at] = value

                by_rows(late, body)

            self.at_home(home)
            self.across_early(j).wait_recv()
            for i in range(self.early // 16):
                at = pl.ds(16 * i, 16)
                total[pl.ds(late + 16 * i, 16)] = early[z, 0, at].astype(F32) + other_early[at].astype(F32)
            for r, result in enumerate(self.results):
                if result[0] == j:
                    self.give(r).start()
                    self.keep(r).start()
        for r in range(len(self.results)):
            self.give(r).wait()
            self.keep(r).wait()
        for j in range(n):
            self.across_early(j).wait_send()

            def sent(o, j=j):
                self.across(j, o).wait_send()

                @pl.when(o != z)
                def _():
                    self.along(j, o, 0, 0).wait_send()
                    self.along_early(j, o, 0, 0).wait_send()

            loop(zn, sent)


class Gains:
    def __init__(self, zn, here, own, got, line, sems):
        self.zn, self.here, self.own, self.got, self.line, self.sems = zn, here, own, got, line, sems

    def swap(self, i):
        d, t, z, x, c = self.here
        device = ((d + 1 - 2 * c, t), (d + 2 - 4 * x, t), (d, 1 - t))[i]
        return remote(self.own, self.got.at[i], self.sems.at[0, i], self.sems.at[1, i], device)

    def along(self, o, slot, down):
        d, t, z, x, c = self.here
        return remote(
            self.own.at[o], self.line.at[slot], self.sems.at[2, o], self.sems.at[3, slot], (d + 4 - 8 * down, t)
        )

    def start(self, rows):
        wide = self.own.shape[2]
        for o in range(self.zn):
            for i, row in enumerate(rows):
                self.own[o, pl.ds(i, 1)] = row[:, pl.ds(o * wide, wide)]
        self.swap(0).start()

    def swapped(self, i):
        self.swap(i).wait()
        self.own[...] += self.got[i]
        if i < 2:
            self.swap(i + 1).start()

    def hop(self, o, slot, down, inner):
        @pl.when(inner)
        def _():
            self.along(o, o, down).wait_recv()
            self.own[o] += self.line[o]

        self.along(o, slot, down).start()

    def steps(self, k, nearest):
        z, zn = self.here[2], self.zn

        @pl.when(z + k < zn)
        def _():
            self.hop(z + k, z + k, 0, z > 0)

        @pl.when(z - k >= 0)
        def _():
            self.hop(z - k, zn if nearest else z - k, 1, z < zn - 1)

    def run(self):
        zn = self.zn

        def step(i, carry):
            self.steps(zn - 1 - i, False)
            return carry

        lax.fori_loop(0, zn - 2, step, 0)
        self.steps(1, True)

    def finish(self, out):
        z, zn = self.here[2], self.zn
        value = self.own[z]

        @pl.when(z > 0)
        def _():
            self.along(z, z, 0).wait_recv()
            self.own[z] += self.line[z]

        @pl.when(z < zn - 1)
        def _():
            self.along(z, zn, 1).wait_recv()
            self.own[z] += self.line[zn]

        out[...] = self.own[z]

        def step(o, carry):
            @pl.when(o != z)
            def _():
                self.along(o, 0, 0).wait_send()

            return carry

        lax.fori_loop(0, zn, step, 0)


def gain_buffers(zn, wide):
    return [
        pltpu.VMEM((zn, 8, wide), F32),
        pltpu.VMEM((3, zn, 8, wide), F32),
        pltpu.VMEM((zn + 1, 8, wide), F32),
        DMA((4, zn + 1)),
    ]


class Total:
    def __init__(self, here, term, from_core, half, from_pair, sems):
        self.here, self.term, self.from_core, self.half, self.from_pair = here, term, from_core, half, from_pair
        self.sems = sems

    def core(self):
        d, t, z, x, c = self.here
        return remote(self.term.at[1 - c], self.from_core, self.sems.at[0], self.sems.at[1], (d + 1 - 2 * c, t))

    def load(self):
        return pltpu.make_async_copy(self.term.at[self.here[4]], self.half, self.sems.at[4])

    def start(self):
        self.core().start()
        self.load().start()

    def pair(self):
        d, t, z, x, c = self.here
        return remote(self.half, self.from_pair, self.sems.at[2], self.sems.at[3], (d, 1 - t))

    def meet(self, loaded=True):
        if loaded:
            self.load().wait()
        self.core().wait_recv()
        block = 16

        def body(i, carry):
            at = pl.ds(pl.multiple_of(i * block, block), block)
            self.half[at] = (self.half[at].astype(F32) + self.from_core[at].astype(F32)).astype(BF16)
            return carry

        lax.fori_loop(0, self.half.shape[0] // block, body, 0)
        self.pair().start()

    def rows(self, at):
        return self.half[at].astype(F32) + self.from_pair[at].astype(F32)

    def finish(self):
        self.core().wait_send()
        self.pair().wait_send()


def total_buffers(tokens, width):
    return [pltpu.VMEM((tokens, width), BF16)] * 3 + [DMA((5,))]


def share(here, src, dst, sems):
    d, t, z, x, c = here
    return (
        pltpu.make_async_copy(src, dst.at[c], sems.at[0]),
        remote(src, dst.at[c], sems.at[1], sems.at[2], (d + 1 - 2 * c, t)),
    )


def gather_attention(zn, early, *refs):
    q, kv, o, gains, tokens, grads, seg = refs[:7]
    qkv_all, o_all, gains_all, tokens_two, grads_two, seg_two = refs[7:13]
    pair_sems = refs[13:16]
    here = place()
    enter(zn, here)
    shared = [
        share(here, src, dst, sems)
        for src, dst, sems in zip((tokens, grads, seg), (tokens_two, grads_two, seg_two), pair_sems)
    ]
    q_half = q.shape[1] // 2
    work = Gather(
        zn,
        here,
        [
            ([(gains, True, 0, gains.shape[2])], gains_all, 0),
            ([(q, False, 0, q_half), (kv, True, q_half, kv.shape[2])], qkv_all, early),
            ([(o, False, 0, o.shape[1] // 2)], o_all, early),
        ],
        refs[16:],
    )
    work.start()
    work.ready(range(3))
    work.start_own(range(3))
    for copies in shared:
        for copy in copies:
            copy.start()
    work.start_early(range(3))
    work.relays(1, range(3))
    for j in range(3):
        work.arrived(j)
    work.finish()
    for copies in shared:
        for copy in copies:
            copy.wait()


def lanes(shape):
    return lax.broadcasted_iota(jnp.int32, shape, 1)


def partner(value):
    half = HEAD_DIM // 2
    wide = 2 * HEAD_DIM
    lower = lax.rem(lanes(value.shape), HEAD_DIM) < half
    return jnp.where(lower, pltpu.roll(value, wide - half, 1), pltpu.roll(value, half, 1))


def allowed_in(column, row):
    shape = (column.shape[0], row.shape[1])
    earlier = lax.broadcasted_iota(jnp.int32, shape, 1) <= lax.broadcasted_iota(jnp.int32, shape, 0)
    return (column == row) & earlier


def softmax_of(queries, keys, allowed):
    scores = jnp.where(allowed, times_transposed(queries, keys) * HEAD_DIM ** (-0.5), -1e30)
    shifted = jnp.exp(scores - jnp.max(scores, axis=-1, keepdims=True))
    return shifted / jnp.sum(shifted, axis=-1, keepdims=True)


def key_value_pairs(pair):
    pair = pair.astype(F32)
    first = lanes(pair.shape) < HEAD_DIM
    key, value = jnp.where(first, pair, 0.0), jnp.where(first, 0.0, pair)
    return [
        part.astype(BF16)
        for part in (key, pltpu.roll(key, HEAD_DIM, 1), pltpu.roll(value, HEAD_DIM, 1), value)
    ]


def attention_block(turned, context, queries_wide, column, row):
    wide = 2 * HEAD_DIM
    allowed = allowed_in(column, row)
    key_one, key_two, value_one, value_two = key_value_pairs(turned[:, queries_wide:])

    def heads(p):
        at = pl.ds(pl.multiple_of(p * wide, wide), wide)
        queries = turned[:, at]
        one = softmax_of(queries, key_one, allowed).astype(BF16)
        two = softmax_of(queries, key_two, allowed).astype(BF16)
        context[:, at] = (product(one, value_one) + product(two, value_two)).astype(BF16)

    loop(queries_wide // wide, heads)


def attention_block_back(turned, grads, back, sums, queries_wide, column, row, cosine, sine):
    wide = 2 * HEAD_DIM
    scale = HEAD_DIM ** (-0.5)
    allowed = allowed_in(column, row)
    key_one, key_two, value_one, value_two = key_value_pairs(turned[:, queries_wide:])
    sums[...] = jnp.zeros_like(sums)

    def heads(p):
        at = pl.ds(pl.multiple_of(p * wide, wide), wide)
        queries, grad = turned[:, at], grads[:, at]
        total = None
        for i, (key, value) in enumerate(((key_one, value_one), (key_two, value_two))):
            probs = softmax_of(queries, key, allowed)
            sums[i] += inner_rows(probs.astype(BF16), grad)
            prob_grad = times_transposed(grad, value)
            delta = jnp.sum(probs * prob_grad, axis=-1, keepdims=True)
            score_grad = (probs * (prob_grad - delta)).astype(BF16)
            term = product(score_grad, key)
            total = term if total is None else total + term
            sums[2 + i] += inner_rows(score_grad, queries)
        total = total * scale
        back[:, at] = (total * cosine - partner(total) * sine).astype(BF16)

    loop(queries_wide // wide, heads)
    value_grad = pltpu.roll(sums[0], HEAD_DIM, 1) + sums[1]
    key_grad = (sums[2] + pltpu.roll(sums[3], HEAD_DIM, 1)) * scale
    turned_back = key_grad * cosine - partner(key_grad) * sine
    back[:, pl.ds(queries_wide, wide)] = jnp.where(
        lanes(value_grad.shape) < HEAD_DIM, turned_back, value_grad
    ).astype(BF16)


def feedforward(zn, early, *refs):
    gate, up, down, tokens, gain, chip_grads = refs[:6]
    chip_tokens, gain_one, qkv_all, o_all, cosines, sines, columns_of, rows_of = refs[6:14]
    gate_all, up_all, down_all, mid_out, normed_out, act_out, gate_grad_out, up_grad_out, back_out = refs[14:23]
    term, normed_one_out, turned_out, context_out = refs[23:27]
    total_refs = refs[27:31]
    normed, out_sems, pair_sems, load_sems, grad_sems, stage_sems, block_sems = refs[31:38]
    here = place()
    c = here[4]
    enter(zn, here)
    total = Total(here, term, *total_refs)
    work = Gather(
        zn,
        here,
        [
            ([(shard, False, 0, shard.shape[1] // 2)], full, early)
            for shard, full in ((down, down_all), (gate, gate_all), (up, up_all))
        ],
        refs[38:],
    )
    count, width = tokens.shape
    columns = gate_all.shape[1]
    block = 256
    blocks = 2 * count // block
    per = count // block
    half = total_refs[1]

    def attention(qkv, o, inputs, normed_one, turned, context, attended):
        queries_wide = context.shape[2]
        wide = 2 * HEAD_DIM

        def place_of(i):
            return lax.rem((1 - c) * per + i, blocks)

        def rows_at(i):
            return pl.ds(pl.multiple_of(place_of(i) * block, block), block)

        def fetch_inputs(i, slot):
            return pltpu.make_async_copy(chip_tokens.at[rows_at(i)], inputs.at[slot], grad_sems.at[slot])

        def stores(i, slot):
            return [
                pltpu.make_async_copy(buffer.at[slot], out.at[rows_at(i)], stage_sems.at[slot, n])
                for n, (buffer, out) in enumerate(
                    ((normed_one, normed_one_out), (turned, turned_out), (context, context_out))
                )
            ]

        def store_term(i, slot):
            return pltpu.make_async_copy(
                attended.at[slot],
                term.at[1 - c, pl.ds(pl.multiple_of(i * block, block), block)],
                block_sems.at[slot],
            )

        fetch_inputs(0, 0).start()
        loads = [
            pltpu.make_async_copy(qkv_all, qkv, load_sems.at[0]),
            pltpu.make_async_copy(o_all, o, load_sems.at[1]),
        ]
        for load in loads:
            load.start()
        for load in loads:
            load.wait()

        def one_block(i):
            slot = lax.rem(i, 2)
            to = rows_at(i)
            fetch_inputs(i, slot).wait()

            @pl.when(i + 1 < blocks)
            def _():
                fetch_inputs(i + 1, 1 - slot).start()

            @pl.when(i > 1)
            def _():
                for copy in stores(i - 2, slot):
                    copy.wait()

            def norm(at):
                value = inputs[slot, at].astype(F32)
                factor = lax.rsqrt(jnp.mean(value * value, axis=-1, keepdims=True) + norm_eps)
                normed_one[slot, at] = (value * factor * gain_one[...]).astype(BF16)

            by_rows(block, norm)
            cosine, sine = cosines[to], sines[to]
            raw = product(normed_one[slot], qkv[...])
            for first in range(0, queries_wide, wide):
                value = raw[:, first : first + wide]
                turned[slot, :, pl.ds(first, wide)] = (value * cosine + partner(value) * sine).astype(BF16)
            value = raw[:, queries_wide:]
            is_key = lanes(value.shape) < HEAD_DIM
            turned[slot, :, pl.ds(queries_wide, wide)] = jnp.where(
                is_key, value * cosine + partner(value) * sine, value
            ).astype(BF16)
            which = place_of(i)
            attention_block(
                turned.at[slot], context.at[slot], queries_wide, columns_of[which], rows_of[which]
            )
            for copy in stores(i, slot):
                copy.start()
            return slot

        def other(i):
            slot = one_block(i)
            attended[slot] = times_transposed(context[slot], o[...]).astype(BF16)
            store_term(i, slot).start()

        def own(i):
            slot = one_block(per + i)
            half[pl.ds(pl.multiple_of(i * block, block), block)] = times_transposed(
                context[slot], o[...]
            ).astype(BF16)

        loop(per, other)
        for i in range(per):
            store_term(i, i % 2).wait()
        total.core().start()
        work.start_early(range(3))
        loop(per, own)
        for i in range(blocks - 2, blocks):
            for copy in stores(i, i % 2):
                copy.wait()

    work.start()
    work.ready(range(3))
    work.start_own([0, 1])
    pl.run_scoped(
        attention,
        pltpu.VMEM(qkv_all.shape, BF16),
        pltpu.VMEM(o_all.shape, BF16),
        pltpu.VMEM((2, block, width), BF16),
        pltpu.VMEM((2, block, width), BF16),
        pltpu.VMEM((2, block, qkv_all.shape[1]), BF16),
        pltpu.VMEM((2, block, o_all.shape[1]), BF16),
        pltpu.VMEM((2, block, width), BF16),
    )
    total.meet(False)
    work.relay(1, [0, 1])
    work.start_own([2])

    def sums(mid):
        total.pair().wait_recv()

        def body(at):
            value = tokens[at].astype(F32) + total.rows(at)
            mid[at] = value
            factor = lax.rsqrt(jnp.mean(value * value, axis=-1, keepdims=True) + norm_eps)
            normed[c, at] = (value * factor * gain[...]).astype(BF16)

        by_rows(count, body)
        save = pltpu.make_async_copy(mid, mid_out, out_sems.at[0])
        save.start()
        for copy in share(here, normed.at[c], normed, pair_sems)[1:]:
            copy.start()
        save.wait()

    def hidden(first, second, silu, slope, up_grad, grads, result, stages, back_stage):
        def fetch_grads(i, slot):
            return pltpu.make_async_copy(
                chip_grads.at[pl.ds(pl.multiple_of(i * block, block), block)], grads.at[slot], grad_sems.at[slot]
            )

        def at_block(i):
            return pl.ds(pl.multiple_of(i * block, block), block)

        fetch_grads(0, 0).start()
        work.arrived(0)
        load = pltpu.make_async_copy(down_all, first, load_sems.at[0])
        load.start()
        load.wait()

        def hidden_block(i):
            slot = lax.rem(i, 2)
            fetch_grads(i, slot).wait()

            @pl.when(i + 1 < blocks)
            def _():
                fetch_grads(i + 1, 1 - slot).start()

            slope[at_block(i)] = product(grads[slot], first[...])

        loop(blocks, hidden_block)
        work.arrived(1)
        load = pltpu.make_async_copy(gate_all, second, load_sems.at[1])
        load.start()
        share(here, normed.at[c], normed, pair_sems)[1].wait()
        save = pltpu.make_async_copy(normed, normed_out, out_sems.at[1])
        save.start()
        load.wait()

        def gate_block(i):
            result[...] = product(normed[i // per, at_block(lax.rem(i, per))], second[...])

            def body(at):
                to = pl.ds(pl.multiple_of(i * block + at.start, 16), at.size)
                gated = result[at]
                grad = slope[to]
                sigmoid = 1.0 / (1.0 + jnp.exp(-gated))
                silu[to] = gated * sigmoid
                up_grad[to] = (grad * gated * sigmoid).astype(BF16)
                slope[to] = grad * (sigmoid * (1.0 + gated * (1.0 - sigmoid)))

            by_rows(block, body)

        loop(blocks, gate_block)
        save_up = pltpu.make_async_copy(up_grad, up_grad_out, out_sems.at[2])
        save_up.start()
        work.relays(3, [2])
        work.arrived(2)
        load = pltpu.make_async_copy(up_all, first, load_sems.at[0])
        load.start()
        load.wait()

        def stores(i, slot):
            to = at_block(i)
            return (
                pltpu.make_async_copy(stages.at[slot, 0], act_out.at[to], stage_sems.at[slot, 0]),
                pltpu.make_async_copy(stages.at[slot, 1], gate_grad_out.at[to], stage_sems.at[slot, 1]),
                pltpu.make_async_copy(
                    back_stage.at[slot], back_out.at[i // per, at_block(lax.rem(i, per))], stage_sems.at[slot, 2]
                ),
            )

        def up_block(i):
            slot = lax.rem(i, 2)

            @pl.when(i > 1)
            def _():
                for copy in stores(i - 2, slot):
                    copy.wait()

            result[...] = product(normed[i // per, at_block(lax.rem(i, per))], first[...])

            def body(at):
                to = pl.ds(pl.multiple_of(i * block + at.start, 16), at.size)
                upward = result[at]
                stages[slot, 0, at] = (silu[to] * upward).astype(BF16)
                stages[slot, 1, at] = (slope[to] * upward).astype(BF16)

            by_rows(block, body)
            value = times_transposed(stages[slot, 1], second[...]) + times_transposed(
                up_grad[at_block(i)], first[...]
            )
            back_stage[slot] = value.astype(BF16)
            for copy in stores(i, slot):
                copy.start()

        loop(blocks, up_block)
        for i in range(max(blocks - 2, 0), blocks):
            for copy in stores(i, i % 2):
                copy.wait()
        save.wait()
        save_up.wait()

    work.relay(2, [0, 1])
    work.relay(1, [2])
    pl.run_scoped(sums, pltpu.VMEM((count, width), F32))
    work.relays(3, [0, 1])
    work.relay(2, [2])
    pl.run_scoped(
        hidden,
        pltpu.VMEM((width, columns), BF16),
        pltpu.VMEM((width, columns), BF16),
        pltpu.VMEM((2 * count, columns), F32),
        pltpu.VMEM((2 * count, columns), F32),
        pltpu.VMEM((2 * count, columns), BF16),
        pltpu.VMEM((2, block, width), BF16),
        pltpu.VMEM((block, columns), F32),
        pltpu.VMEM((2, 2, block, columns), BF16),
        pltpu.VMEM((2, block, width), BF16),
    )
    work.finish()
    total.finish()


def fetch(pairs, sems):
    copies = [pltpu.make_async_copy(src, dst, sems.at[i]) for i, (src, dst) in enumerate(pairs)]
    for copy in copies:
        copy.start()
    return copies


def scatter_feedforward(zn, early, *refs):
    normed, gate_grad, chip_grads, activated, back_term, down_all, mid_in, gain = refs[:8]
    turned_all, o_all, qkv_all, cosines, sines, columns_of, rows_of = refs[8:15]
    gate_out, down_out, out, mid_grad_out, branch_out, gain_out, qkv_back, in_term = refs[15:23]
    gate, down, out_term = refs[23:26]
    buffers, refs = refs[26 : 26 + 2 * SCATTER_BUFFERS], refs[26 + 2 * SCATTER_BUFFERS :]
    back_refs, out_refs = refs[:4], refs[4:8]
    fetch_sems, out_sems, pair_sems, weight_sems, stage_sems, block_sems, back_sems = refs[8:15]
    branch, out_rows = back_refs[0], out_refs[0]
    here = place()
    c = here[4]
    chip, width = chip_grads.shape
    enter(zn, here)
    back = Total(here, back_term, *back_refs)
    front = Total(here, out_term, *out_refs)
    work = Scatter(
        zn,
        here,
        early,
        [
            (
                term,
                buffers[SCATTER_BUFFERS * j : SCATTER_BUFFERS * (j + 1)],
                [(result, False, 0, result.shape[1] // 2)],
            )
            for j, (term, result) in enumerate(((down, down_out), (gate, gate_out)))
        ],
        refs[15:],
    )
    back.start()

    def out_terms(right_one, weights, stages):
        block = weights.shape[1]

        def fetch_weights(i, slot):
            return pltpu.make_async_copy(
                down_all.at[pl.ds(pl.multiple_of(i * block, block), block)], weights.at[slot], weight_sems.at[slot]
            )

        def stores(i, slot):
            to = pl.ds(pl.multiple_of(i * block, block), block)
            return [
                pltpu.make_async_copy(
                    stages.at[slot, pl.ds(half * (chip // 2), chip // 2)],
                    out_term.at[half, :, to],
                    stage_sems.at[slot, half],
                )
                for half in range(2)
            ]

        fetch_weights(0, 0).start()

        def step(i):
            slot = lax.rem(i, 2)
            fetch_weights(i, slot).wait()

            @pl.when(i + 1 < width // block)
            def _():
                fetch_weights(i + 1, 1 - slot).start()

            @pl.when(i > 1)
            def _():
                for copy in stores(i - 2, slot):
                    copy.wait()

            stages[slot] = times_transposed(right_one[...], weights[slot]).astype(BF16)
            for copy in stores(i, slot):
                copy.start()

        loop(width // block, step)
        for i in range(width // block - 2, width // block):
            for copy in stores(i, i % 2):
                copy.wait()

    def terms(left_one, right_one, left_two, right_two, stage, weights, stages):
        copies = fetch(
            (
                (chip_grads, left_one),
                (activated, right_one),
                (normed, left_two),
                (gate_grad, right_two),
            ),
            fetch_sems,
        )
        copies[0].wait()
        copies[1].wait()
        work.make(0, left_one, right_one, stage, back.meet)
        copies[2].wait()
        copies[3].wait()
        work.make(1, left_two, right_two, stage)
        out_terms(right_one, weights, stages)
        front.start()

    pl.run_scoped(
        terms,
        pltpu.VMEM(chip_grads.shape, BF16),
        pltpu.VMEM(activated.shape, BF16),
        pltpu.VMEM(normed.shape, BF16),
        pltpu.VMEM(gate_grad.shape, BF16),
        pltpu.VMEM((2,) + down.shape[1:], BF16),
        pltpu.VMEM((2, 256, down.shape[2]), BF16),
        pltpu.VMEM((2, chip, 256), BF16),
    )

    def sums(mid, mid_grad, grads):
        copies = fetch(
            (
                (mid_in, mid),
                (chip_grads.at[pl.ds(pl.multiple_of(c * (chip // 2), 16), chip // 2)], grads),
            ),
            fetch_sems,
        )
        work.late_hops(0)
        front.meet()
        for copy in copies:
            copy.wait()
        gain_out[...] = jnp.zeros_like(gain_out)

        def body_gain(at):
            value = mid[at]
            factor = lax.rsqrt(jnp.mean(value * value, axis=-1, keepdims=True) + norm_eps)
            gain_out[...] += jnp.sum(back.half[at].astype(F32) * (value * factor), axis=0, keepdims=True)

        by_rows(chip // 2, body_gain)
        back.pair().wait_recv()

        def body(at):
            value = mid[at]
            factor = lax.rsqrt(jnp.mean(value * value, axis=-1, keepdims=True) + norm_eps)
            scaled = back.rows(at) * gain[...]
            result = (
                grads[at].astype(F32)
                + factor * scaled
                - value * (factor * factor * factor) * jnp.mean(scaled * value, axis=-1, keepdims=True)
            )
            mid_grad[at] = result
            branch[at] = result.astype(BF16)

        by_rows(chip // 2, body)
        save = pltpu.make_async_copy(mid_grad, mid_grad_out, out_sems.at[0])
        save.start()
        for copy in share(here, branch, branch_out, pair_sems):
            copy.start()
        work.early_home(1)
        save.wait()

    pl.run_scoped(
        sums,
        pltpu.VMEM((chip // 2, width), F32),
        pltpu.VMEM((chip // 2, width), F32),
        pltpu.VMEM((chip // 2, width), BF16),
    )

    def attention(o, qkv, inputs, turned, grads, backs, terms_out, cosine, sine, accumulators):
        block = inputs.shape[1]
        blocks = chip // block
        per = blocks // 2
        queries_wide = o.shape[1]

        def rows_at(i):
            return pl.ds(pl.multiple_of(i * block, block), block)

        def fetches(i, slot):
            sources = (
                (branch_out.at[i // per, rows_at(lax.rem(i, per))], inputs),
                (turned_all.at[rows_at(i)], turned),
                (cosines.at[rows_at(i)], cosine),
                (sines.at[rows_at(i)], sine),
            )
            return [
                pltpu.make_async_copy(source, buffer.at[slot], block_sems.at[slot, n])
                for n, (source, buffer) in enumerate(sources)
            ]

        def stores(i, slot):
            return [
                pltpu.make_async_copy(backs.at[slot], qkv_back.at[rows_at(i)], back_sems.at[slot, 0]),
                pltpu.make_async_copy(
                    terms_out.at[slot], in_term.at[i // per, rows_at(lax.rem(i, per))], back_sems.at[slot, 1]
                ),
            ]

        loads = fetch(((o_all, o), (qkv_all, qkv)), fetch_sems)
        for copy in share(here, branch, branch_out, pair_sems):
            copy.wait()
        for copy in fetches(0, 0):
            copy.start()
        for load in loads:
            load.wait()

        def step(i):
            slot = lax.rem(i, 2)
            work.share_of_hops(1, i, blocks)
            for copy in fetches(i, slot):
                copy.wait()

            @pl.when(i + 1 < blocks)
            def _():
                for copy in fetches(i + 1, 1 - slot):
                    copy.start()

            @pl.when(i > 1)
            def _():
                for copy in stores(i - 2, slot):
                    copy.wait()

            grads[...] = product(inputs[slot], o[...]).astype(BF16)
            attention_block_back(
                turned.at[slot],
                grads,
                backs.at[slot],
                accumulators,
                queries_wide,
                columns_of[i],
                rows_of[i],
                cosine[slot],
                sine[slot],
            )
            terms_out[slot] = times_transposed(backs[slot], qkv[...]).astype(BF16)
            for copy in stores(i, slot):
                copy.start()

        loop(blocks, step)
        for i in range(blocks - 2, blocks):
            for copy in stores(i, i % 2):
                copy.wait()

    block = rows_of.shape[2]
    qkv_wide = qkv_all.shape[1]
    pl.run_scoped(
        attention,
        pltpu.VMEM(o_all.shape, BF16),
        pltpu.VMEM(qkv_all.shape, BF16),
        pltpu.VMEM((2, block, width), BF16),
        pltpu.VMEM((2, block, qkv_wide), BF16),
        pltpu.VMEM((block, o_all.shape[1]), BF16),
        pltpu.VMEM((2, block, qkv_wide), BF16),
        pltpu.VMEM((2, block, width), BF16),
        pltpu.VMEM((2, block, 2 * HEAD_DIM), F32),
        pltpu.VMEM((2, block, 2 * HEAD_DIM), F32),
        pltpu.VMEM((4, block, 2 * HEAD_DIM), F32),
    )

    def output(mid):
        load = fetch(((mid_in, mid),), fetch_sems)[0]
        front.pair().wait_recv()
        load.wait()

        def body_out(at):
            out_rows[at] = (mid[at] + front.rows(at)).astype(BF16)

        by_rows(chip // 2, body_out)

    pl.run_scoped(output, pltpu.VMEM((chip // 2, width), F32))
    save_out = pltpu.make_async_copy(out_rows, out, out_sems.at[1])
    save_out.start()
    work.finish()
    back.finish()
    front.finish()
    save_out.wait()


def scatter_attention(zn, early, *refs):
    normed, qkv_grad, branch, context, normed_two, up_grad, term, mid_grad_in, tokens, gain, two_sum = refs[:11]
    q_out, kv_out, o_out, up_out, in_grad, gain_out, qkv, o, up = refs[11:20]
    buffers, refs = refs[20 : 20 + 3 * SCATTER_BUFFERS], refs[20 + 3 * SCATTER_BUFFERS :]
    total_refs, gain_refs = refs[:4], refs[4:8]
    fetch_sems, out_sems, one_sum = refs[8:11]
    rows_out = total_refs[0]
    here = place()
    enter(zn, here)
    total = Total(here, term, *total_refs)
    q_half = q_out.shape[1] // 2
    work = Scatter(
        zn,
        here,
        early,
        [
            (up, buffers[:SCATTER_BUFFERS], [(up_out, False, 0, up_out.shape[1] // 2)]),
            (o, buffers[SCATTER_BUFFERS : 2 * SCATTER_BUFFERS], [(o_out, False, 0, o_out.shape[1] // 2)]),
            (
                qkv,
                buffers[2 * SCATTER_BUFFERS :],
                [(q_out, False, 0, q_half), (kv_out, True, q_half, kv_out.shape[2])],
            ),
        ],
        refs[11:],
    )
    gains = Gains(zn, here, *gain_refs)
    total.start()

    def terms(left_one, right_one, left_two, right_two, right_three, stage):
        copies = fetch(
            (
                (normed_two, left_one),
                (up_grad, right_one),
                (branch, left_two),
                (context, right_two),
                (qkv_grad, right_three),
            ),
            fetch_sems,
        )
        copies[0].wait()
        copies[1].wait()
        work.make(0, left_one, right_one, stage, total.meet)
        last = pltpu.make_async_copy(normed, left_one, fetch_sems.at[5])
        last.start()
        one_sum[...] = jnp.zeros_like(one_sum)

        def body_gain(at):
            value = tokens[at].astype(F32)
            factor = lax.rsqrt(jnp.mean(value * value, axis=-1, keepdims=True) + norm_eps)
            one_sum[...] += jnp.sum(total.half[at].astype(F32) * (value * factor), axis=0, keepdims=True)

        by_rows(tokens.shape[0], body_gain)
        gains.start([one_sum, two_sum])
        gains.swapped(0)
        copies[2].wait()
        copies[3].wait()
        work.make(1, left_two, right_two, stage)
        copies[4].wait()
        last.wait()
        work.make(2, left_one, right_three, stage)

    pl.run_scoped(
        terms,
        pltpu.VMEM(normed.shape, BF16),
        pltpu.VMEM(up_grad.shape, BF16),
        pltpu.VMEM(branch.shape, BF16),
        pltpu.VMEM(context.shape, BF16),
        pltpu.VMEM(qkv_grad.shape, BF16),
        pltpu.VMEM((2,) + up.shape[1:], BF16),
    )

    def sums(mid_grad):
        copies = fetch(((mid_grad_in, mid_grad),), fetch_sems)
        work.late_hops(0)
        gains.swapped(1)
        work.late_hops(1)
        gains.swapped(2)
        gains.run()
        work.late_hops(2)
        gains.finish(gain_out)
        for copy in copies:
            copy.wait()
        total.pair().wait_recv()

        def body(at):
            value = tokens[at].astype(F32)
            factor = lax.rsqrt(jnp.mean(value * value, axis=-1, keepdims=True) + norm_eps)
            scaled = total.rows(at) * gain[...]
            rows_out[at] = (
                mid_grad[at]
                + factor * scaled
                - value * (factor * factor * factor) * jnp.mean(scaled * value, axis=-1, keepdims=True)
            ).astype(BF16)

        by_rows(tokens.shape[0], body)
        save = pltpu.make_async_copy(rows_out, in_grad, out_sems.at[0])
        save.start()
        save.wait()

    pl.run_scoped(sums, pltpu.VMEM(mid_grad_in.shape, F32))
    work.finish()
    total.finish()


def call(kernel, name, collective_id, operands, specs, outs, out_specs, scratch, order=None):
    results = pl.pallas_call(
        kernel,
        out_shape=[jax.ShapeDtypeStruct(shape, dtype) for shape, dtype in outs],
        in_specs=specs,
        out_specs=out_specs,
        scratch_shapes=scratch,
        name=name,
        compiler_params=pltpu.CompilerParams(
            collective_id=collective_id, has_side_effects=True, vmem_limit_bytes=58 << 20
        ),
    )(*operands)
    return results if order is None else [results[i] for i in order]


def rotate(vectors, cosine, sine_rows):
    half = vectors.shape[-1] // 2
    first, second = vectors[..., :half], vectors[..., half:]
    return jnp.concatenate(
        [first * cosine - second * sine_rows, second * cosine + first * sine_rows], axis=-1
    )


def product(one, two):
    return jnp.dot(one, two, preferred_element_type=F32)


def times_transposed(one, two):
    return lax.dot_general(one, two, (((1,), (1,)), ((), ())), preferred_element_type=F32)


def inner_rows(one, two):
    return lax.dot_general(one, two, (((0,), (0,)), ((), ())), preferred_element_type=F32)


def einsum(form, one, two):
    return jnp.einsum(form, one, two, preferred_element_type=F32)


def halves(weight):
    rows, columns = weight.shape
    return weight.reshape(rows, 2, columns // 2).transpose(1, 0, 2)


def joined(pair):
    return jnp.concatenate([pair[0], pair[1]], axis=1)


def local(
    dp,
    tokens,
    seg_ids,
    q_weight,
    k_weight,
    v_weight,
    o_weight,
    attn_gain,
    gate_weight,
    up_weight,
    down_weight,
    mlp_gain,
    out_grad,
):
    zn = dp // 4
    units = zn * 2
    count, width = tokens.shape
    rows = q_weight.shape[0]
    blocks, block_rows = 2 * seg_ids.shape[0], seg_ids.shape[1]
    q_half, kv_half = q_weight.shape[1] // 2, k_weight.shape[1] // 2
    ff_half = gate_weight.shape[1] // 2
    qkv_half = q_half + 2 * kv_half
    heads, groups = q_half // HEAD_DIM, kv_half // HEAD_DIM
    early = 2 * rows // 48 * 8
    early_sums = max(16, 2 * rows // 128 * 16)

    kv_shard = jnp.concatenate([halves(k_weight), halves(v_weight)], axis=2)
    gain_rows = jnp.zeros((8, 128), F32)
    gain_rows = gain_rows.at[0, :rows].set(attn_gain.astype(F32)).at[1, :rows].set(mlp_gain.astype(F32))
    gain_shard = jnp.stack([gain_rows, gain_rows])

    qkv_full, o_full, gains, tokens_two, grads_two, seg_two = call(
        functools.partial(gather_attention, zn, early),
        "gather_attention",
        0,
        (q_weight, kv_shard, o_weight.T, gain_shard, tokens, out_grad, seg_ids),
        [VMEM] * 7,
        [
            ((width, qkv_half), BF16),
            ((width, q_half), BF16),
            ((units * 16, 128), F32),
            ((2, count, width), BF16),
            ((2, count, width), BF16),
            ((2,) + seg_ids.shape, jnp.int32),
        ],
        [ANY] * 6,
        [DMA((3,))] * 3 + gather_sems(3, 4, zn),
    )
    gains = gains.reshape(dp, 8, 128)[:, :, :rows]
    gain_one, gain_two = gains[:, 0].reshape(1, width), gains[:, 1].reshape(1, width)
    chip = 2 * count
    tokens_chip = tokens_two.reshape(chip, width)
    grads_chip = grads_two.reshape(chip, width)
    segment = seg_two.reshape(blocks, block_rows)

    order = jnp.arange(block_rows, dtype=jnp.int32)
    same = segment[:, :, None] == segment[:, None, :]
    position = jnp.sum((same & (order[None, :] < order[:, None])).astype(jnp.int32), axis=2)
    inverse = 1.0 / 10000.0 ** (jnp.arange(0, HEAD_DIM, 2, dtype=F32) / HEAD_DIM)
    angles = position.astype(F32).reshape(chip, 1) * jnp.tile(inverse, 4)
    sign = jnp.tile(jnp.repeat(jnp.array([-1.0, 1.0], F32), HEAD_DIM // 2), 2)
    cosines, sines = jnp.cos(angles), jnp.sin(angles) * sign

    mid, normed_two, activated, gate_grad, up_grad, back_term, down_full, normed, turned, context = call(
        functools.partial(feedforward, zn, early),
        "feedforward",
        1,
        (
            gate_weight,
            up_weight,
            down_weight.T,
            tokens,
            gain_two,
            grads_chip,
            tokens_chip,
            gain_one,
            qkv_full,
            o_full,
            cosines,
            sines,
            segment[:, :, None],
            segment[:, None, :],
        ),
        [VMEM] * 5 + [ANY] * 2 + [VMEM] + [ANY] * 2 + [VMEM] * 4,
        [((width, ff_half), BF16)] * 3
        + [((count, width), F32), ((2, count, width), BF16)]
        + [((chip, ff_half), BF16)] * 3
        + [((2, count, width), BF16)] * 2
        + [((chip, width), BF16), ((chip, qkv_half), BF16), ((chip, q_half), BF16)],
        [ANY] * 13,
        total_buffers(count, width)
        + [pltpu.VMEM((2, count, width), BF16), DMA((3,)), DMA((3,)), DMA((2,)), DMA((2,)), DMA((2, 3)), DMA((2,))]
        + gather_sems(3, 3, zn),
        order=(3, 4, 5, 6, 7, 8, 2, 10, 11, 12),
    )
    normed_two = normed_two.reshape(chip, width)

    gate_sum, down_sum, out, mid_grad, branch, gain_two_grad, qkv_back, in_term = call(
        functools.partial(scatter_feedforward, zn, early_sums),
        "scatter_feedforward",
        2,
        (
            normed_two,
            gate_grad,
            grads_chip,
            activated,
            back_term,
            down_full,
            mid,
            gain_two,
            turned,
            o_full,
            qkv_full,
            cosines,
            sines,
            segment[:, :, None],
            segment[:, None, :],
        ),
        [ANY] * 7 + [VMEM] + [ANY] * 5 + [VMEM] * 2,
        [((rows, 2 * ff_half), F32)] * 2
        + [
            ((count, width), BF16),
            ((count, width), F32),
            ((2, count, width), BF16),
            ((1, width), F32),
            ((chip, qkv_half), BF16),
            ((2, count, width), BF16),
        ]
        + [((zn, 4 * rows, ff_half), BF16)] * 2
        + [((2, count, width), BF16)],
        [ANY] * 5 + [VMEM] + [ANY] * 5,
        scatter_buffers([(2 * rows, ff_half)] * 2, early_sums, zn)
        + total_buffers(count, width) * 2
        + [DMA((4,)), DMA((2,)), DMA((3,)), DMA((2,)), DMA((2, 2)), DMA((2, 4)), DMA((2, 2))]
        + scatter_sems(2, 2, zn),
        order=range(8),
    )
    branch = branch.reshape(chip, width)

    q_sum, kv_sum, o_sum, up_sum, in_grad, gain_sums = call(
        functools.partial(scatter_attention, zn, early_sums),
        "scatter_attention",
        3,
        (
            normed,
            qkv_back,
            branch,
            context,
            normed_two,
            up_grad,
            in_term,
            mid_grad,
            tokens,
            gain_one,
            gain_two_grad,
        ),
        [ANY] * 8 + [VMEM] * 3,
        [
            ((rows, 2 * q_half), F32),
            ((2, rows, 2 * kv_half), F32),
            ((rows, 2 * q_half), F32),
            ((rows, 2 * ff_half), F32),
            ((count, width), BF16),
            ((8, 4 * rows), F32),
            ((zn, 4 * rows, qkv_half), BF16),
            ((zn, 4 * rows, q_half), BF16),
            ((zn, 4 * rows, ff_half), BF16),
        ],
        [ANY] * 5 + [VMEM] + [ANY] * 3,
        scatter_buffers([(2 * rows, ff_half), (2 * rows, q_half), (2 * rows, qkv_half)], early_sums, zn)
        + total_buffers(count, width)
        + gain_buffers(zn, 4 * rows)
        + [DMA((6,)), DMA((1,)), pltpu.VMEM((1, width), F32)]
        + scatter_sems(3, 4, zn),
        order=range(6),
    )
    gain_grads = lax.dynamic_slice_in_dim(gain_sums, lax.rem(lax.axis_index("dp"), 4) * rows, rows, 1)
    return (
        out,
        in_grad,
        q_sum,
        joined(kv_sum[:, :, :kv_half]),
        joined(kv_sum[:, :, kv_half:]),
        o_sum.T,
        gain_grads[0],
        gate_sum,
        up_sum,
        down_sum.T,
        gain_grads[1],
    )


def solution(mesh):
    arguments = (
        P("dp", None),
        P("dp", None),
        P("dp", "tensor"),
        P("dp", "tensor"),
        P("dp", "tensor"),
        P("tensor", "dp"),
        P("dp"),
        P("dp", "tensor"),
        P("dp", "tensor"),
        P("tensor", "dp"),
        P("dp"),
        P("dp", None),
    )
    results = (
        P("dp", None),
        P("dp", None),
        P("dp", "tensor"),
        P("dp", "tensor"),
        P("dp", "tensor"),
        P("tensor", "dp"),
        P("dp"),
        P("dp", "tensor"),
        P("dp", "tensor"),
        P("tensor", "dp"),
        P("dp"),
    )
    return jax.shard_map(
        functools.partial(local, mesh.shape["dp"]),
        mesh=mesh,
        in_specs=arguments,
        out_specs=results,
        check_vma=False,
    )
```

profile of v0, /device:TPU:0, one launch (start us, length us, event | category | flops | bytes accessed | tf_op | source)
XLA Modules:
  0.0 581.5 jit_solution(8131249409892712735)
XLA Ops:
  0.6 1.8 copy.47
  2.4 0.0 copy-start.7
  2.4 0.9 copy.43
  3.3 0.1 copy.44
  3.5 0.9 copy.45
  4.3 0.1 copy.46
  4.5 0.7 pad_maximum_fusion.refs_1_
  5.2 0.7 bitcast_convert_fusion
  5.8 0.7 bitcast_convert_fusion.1
  6.5 0.6 pad_maximum_fusion.3.refs_3_
  7.1 0.0 copy-start.5
  7.1 63.4 %gather_attention.1 = (bf16[2048,640]{1,0:T(8,128)(2,1)}, bf16[2048,512]{1,0:T(8,128)(2,1)}, f32[128,128]{1,0:T(8,128)}, bf16[2,512,2048]{2,1,0:T(8,128)(2,1)}, ...) custom-call(bf16[128,1024]{1,0:T(8,128)(2,1)} %refs_0_.2, bf16[2,128,128]{2,1,0:T(8,128)(2,1)} %pad_maximum_fusion.refs_1_, ...), custom_call_target="tpu_custom_call" | custom-call | tf_op jit(solution)/shard_map/gather_attention/pallas_call | solution.py:1499
  70.6 0.7 eq.15
  71.3 0.4 convert_reduce_fusion
  71.7 0.1 mul.32
  71.8 0.0 copy-done.7
  71.8 0.1 broadcast_in_dim.2
  71.9 0.1 tile.14
  72.0 0.1 mul.35
  72.1 3.0 fusion
  75.1 1.8 broadcast_in_dim_reshape.12.refs_12_.refs_13_
  76.9 1.3 broadcast_in_dim_reshape.5.refs_13_.refs_14_
  78.2 1.5 slice_bitcast_fusion.4
  79.7 0.0 copy-done.5
  79.7 1.1 copy.42
  80.9 220.3 %feedforward.1 = (bf16[2048,1408]{1,0:T(8,128)(2,1)}, bf16[2048,1408]{1,0:T(8,128)(2,1)}, bf16[2048,1408]{1,0:T(8,128)(2,1)}, f32[512,2048]{1,0:T(8,128)}, bf16[...) custom-call(bf16[128,2816]{1,0:T(8,128)(2,1)} %refs_0_.3, ...), custom_call_target="tpu_custom_call" | custom-call | tf_op jit(solution)/shard_map/feedforward/pallas_call | solution.py:1499
  301.2 136.9 %scatter_feedforward.1 = (f32[128,2816]{1,0:T(8,128)}, f32[128,2816]{1,0:T(8,128)}, bf16[512,2048]{1,0:T(8,128)(2,1)}, f32[512,2048]{1,0:T(8,128)}, bf16[2,512,2...) custom-call(bf16[1024,2048]{1,0:T(8,128)(2,1)} %bitcast.45, ...), custom_call_target="tpu_custom_call" | custom-call | tf_op jit(solution)/shard_map/scatter_feedforward/pallas_call | solution.py:1499
  438.1 0.0 copy-start.3
  438.1 129.7 %scatter_attention.1 = (f32[128,1024]{1,0:T(8,128)}, f32[2,128,128]{2,1,0:T(8,128)}, f32[128,1024]{1,0:T(8,128)}, f32[128,2816]{1,0:T(8,128)}, bf16[512,2048]{1,...) custom-call(bf16[1024,2048]{1,0:T(8,128)(2,1)} %get-tuple-element.79, ...), custom_call_target="tpu_custom_call" | custom-call | tf_op jit(solution)/shard_map/scatter_attention/pallas_call | solution.py:1499
  567.9 0.0 copy-start
  567.9 1.2 slice_bitcast_fusion.1
  569.1 0.8 pad_maximum_fusion.1
  569.8 2.0 copy.52
  571.9 0.7 constant_dynamic-slice_fusion
  572.5 0.5 slice_bitcast_fusion.6
  573.1 0.0 copy-done.3
  573.1 1.5 copy.53
  574.6 0.0 copy-start.1
  574.6 0.0 copy-done
  574.6 1.3 copy.63
  575.9 1.0 copy-done.1
  577.0 0.0 copy-start.6
  577.0 0.0 copy-start.2
  577.0 1.3 copy.64
  578.3 0.1 copy-done.6
  578.3 0.0 copy-start.4
  578.3 0.8 copy.65
  579.1 0.1 copy-done.2
  579.2 1.1 copy.66
  580.3 0.0 copy-done.4
  580.3 1.1 copy.67
  (7 shorter events, 0.1 us)
Async XLA Ops:
  2.4 69.4 %copy-start.7 = (f32[2]{0:T(128)S(1)}, f32[2]{0:T(128)}, u32[]{:S(2)}) copy-start(f32[2]{0:T(128)} %constant.84.clone) | copy-start | bytes 28
  7.1 72.6 %copy-start.5 = (bf16[2816,128]{1,0:T(8,128)(2,1)S(1)}, bf16[2816,128]{1,0:T(8,128)(2,1)}, u32[]{:S(2)}) copy-start(bf16[2816,128]{1,0:T(8,128)(2,1)} %param.26) | copy-start | bytes 2162692
  438.1 134.9 %copy-start.3 = (f32[128,2816]{1,0:T(8,128)S(1)}, f32[128,2816]{1,0:T(8,128)}, u32[]{:S(2)}) copy-start(f32[128,2816]{1,0:T(8,128)} %get-tuple-element.94) | copy-start | bytes 4325380
  567.9 6.7 %copy-start = (bf16[512,2048]{1,0:T(8,128)(2,1)S(1)}, bf16[512,2048]{1,0:T(8,128)(2,1)}, u32[]{:S(2)}) copy-start(bf16[512,2048]{1,0:T(8,128)(2,1)} %get-tuple-element.151) | copy-start | bytes 6291460
  574.6 2.3 copy-start.1
  577.0 1.4 copy-start.6
  577.0 2.3 copy-start.2
  578.3 2.0 copy-start.4
where the time goes:
time: 583 us; the launch traced here: 581 us
  Pallas kernels  550 us (94%)
  local copies, waits for them, and re-layouts  23.4 us (4%)
  other arithmetic  6.89 us (1%)
    pallas_call x4, Pallas kernels, call(): pl.pallas_call(kernel, out_shape=[jax.ShapeDtypeStruct(shape, dtype) for...  550 us
    unnamed x28, local copies, waits for them, and re-layouts  15.1 us

commit v1 on v0

--- a/solution.py
+++ b/solution.py
@@ -728,43 +728,6 @@
     )
 
 
-def gather_attention(zn, early, *refs):
-    q, kv, o, gains, tokens, grads, seg = refs[:7]
-    qkv_all, o_all, gains_all, tokens_two, grads_two, seg_two = refs[7:13]
-    pair_sems = refs[13:16]
-    here = place()
-    enter(zn, here)
-    shared = [
-        share(here, src, dst, sems)
-        for src, dst, sems in zip((tokens, grads, seg), (tokens_two, grads_two, seg_two), pair_sems)
-    ]
-    q_half = q.shape[1] // 2
-    work = Gather(
-        zn,
-        here,
-        [
-            ([(gains, True, 0, gains.shape[2])], gains_all, 0),
-            ([(q, False, 0, q_half), (kv, True, q_half, kv.shape[2])], qkv_all, early),
-            ([(o, False, 0, o.shape[1] // 2)], o_all, early),
-        ],
-        refs[16:],
-    )
-    work.start()
-    work.ready(range(3))
-    work.start_own(range(3))
-    for copies in shared:
-        for copy in copies:
-            copy.start()
-    work.start_early(range(3))
-    work.relays(1, range(3))
-    for j in range(3):
-        work.arrived(j)
-    work.finish()
-    for copies in shared:
-        for copy in copies:
-            copy.wait()
-
-
 def lanes(shape):
     return lax.broadcasted_iota(jnp.int32, shape, 1)
 
@@ -776,10 +739,17 @@
     return jnp.where(lower, pltpu.roll(value, wide - half, 1), pltpu.roll(value, half, 1))
 
 
-def allowed_in(column, row):
-    shape = (column.shape[0], row.shape[1])
-    earlier = lax.broadcasted_iota(jnp.int32, shape, 1) <= lax.broadcasted_iota(jnp.int32, shape, 0)
-    return (column == row) & earlier
+def same_segment(row):
+    count = row.shape[1]
+    wide = jnp.broadcast_to(row, (count, count))
+    before = lax.broadcasted_iota(jnp.int32, wide.shape, 1) < lax.broadcasted_iota(jnp.int32, wide.shape, 0)
+    return wide == wide.T, before
+
+
+def allowed_in(row):
+    same, before = same_segment(row)
+    here = lax.broadcasted_iota(jnp.int32, same.shape, 1) == lax.broadcasted_iota(jnp.int32, same.shape, 0)
+    return same & (before | here)
 
 
 def softmax_of(queries, keys, allowed):
@@ -798,9 +768,9 @@
     ]
 
 
-def attention_block(turned, context, queries_wide, column, row):
+def attention_block(turned, context, queries_wide, row):
     wide = 2 * HEAD_DIM
-    allowed = allowed_in(column, row)
+    allowed = allowed_in(row)
     key_one, key_two, value_one, value_two = key_value_pairs(turned[:, queries_wide:])
 
     def heads(p):
@@ -813,10 +783,10 @@
     loop(queries_wide // wide, heads)
 
 
-def attention_block_back(turned, grads, back, sums, queries_wide, column, row, cosine, sine):
+def attention_block_back(turned, grads, back, sums, queries_wide, row, cosine, sine):
     wide = 2 * HEAD_DIM
     scale = HEAD_DIM ** (-0.5)
-    allowed = allowed_in(column, row)
+    allowed = allowed_in(row)
     key_one, key_two, value_one, value_two = key_value_pairs(turned[:, queries_wide:])
     sums[...] = jnp.zeros_like(sums)
 
@@ -845,31 +815,97 @@
     ).astype(BF16)
 
 
-def feedforward(zn, early, *refs):
-    gate, up, down, tokens, gain, chip_grads = refs[:6]
-    chip_tokens, gain_one, qkv_all, o_all, cosines, sines, columns_of, rows_of = refs[6:14]
-    gate_all, up_all, down_all, mid_out, normed_out, act_out, gate_grad_out, up_grad_out, back_out = refs[14:23]
-    term, normed_one_out, turned_out, context_out = refs[23:27]
-    total_refs = refs[27:31]
-    normed, out_sems, pair_sems, load_sems, grad_sems, stage_sems, block_sems = refs[31:38]
+def forward(zn, early, *refs):
+    q, kv, o_shard, gains, tokens, grads, seg, gate, up, down, inverse, sign = refs[:12]
+    qkv_all, o_all, gains_all, chip_tokens, chip_grads, seg_all = refs[12:18]
+    gate_all, up_all, down_all, mid_out, normed_out, act_out, gate_grad_out, up_grad_out, back_out = refs[18:27]
+    term, normed_one_out, turned_out, context_out, cosines_out, sines_out, gain_out = refs[27:34]
+    total_refs = refs[34:38]
+    normed, out_sems, pair_sems, load_sems, grad_sems, stage_sems, block_sems = refs[38:45]
+    cosines, sines, seg_pair, gain_tiles, gain_rows, swap_sems, seg_sems = refs[45:52]
     here = place()
     c = here[4]
     enter(zn, here)
     total = Total(here, term, *total_refs)
+    q_half = q.shape[1] // 2
     work = Gather(
         zn,
         here,
         [
+            ([(gains, True, 0, gains.shape[2])], gains_all, 0),
+            ([(q, False, 0, q_half), (kv, True, q_half, kv.shape[2])], qkv_all, early),
+            ([(o_shard, False, 0, o_shard.shape[1] // 2)], o_all, early),
+        ]
+        + [
             ([(shard, False, 0, shard.shape[1] // 2)], full, early)
             for shard, full in ((down, down_all), (gate, gate_all), (up, up_all))
         ],
-        refs[38:],
+        refs[52:],
     )
     count, width = tokens.shape
     columns = gate_all.shape[1]
-    block = 256
+    block = seg.shape[1]
     blocks = 2 * count // block
     per = count // block
+    attention_set = [0, 1, 2]
+    swap = remote(seg, seg_pair.at[c], seg_sems.at[0], seg_sems.at[1], (here[0] + 1 - 2 * c, here[1]))
+    swap.start()
+    seg_pair[c] = seg[...]
+    work.start()
+    work.ready(attention_set)
+    work.start_own(attention_set)
+    shared = [
+        share(here, src, dst, swap_sems.at[n])
+        for n, (src, dst) in enumerate(((tokens, chip_tokens), (grads, chip_grads)))
+    ]
+    for copies in shared:
+        for copy in copies:
+            copy.start()
+    work.ready([5])
+    work.start_own([5])
+    swap.wait()
+    for i in range(blocks):
+        row = seg_pair[i // per, pl.ds(i % per, 1)]
+        same, before = same_segment(row)
+        position = jnp.sum(jnp.where(same & before, 1.0, 0.0), axis=-1, keepdims=True)
+        angles = position * inverse[...]
+        cosines[pl.ds(i * block, block)] = jnp.cos(angles)
+        sines[pl.ds(i * block, block)] = jnp.sin(angles) * sign[...]
+    saves = [
+        pltpu.make_async_copy(src, dst, seg_sems.at[2 + n])
+        for n, (src, dst) in enumerate(((cosines, cosines_out), (sines, sines_out), (seg_pair, seg_all)))
+    ]
+    for copy in saves:
+        copy.start()
+    work.start_early([1, 2])
+    work.relay(1, attention_set)
+    work.start_early([5])
+    work.ready([3])
+    work.start_own([3])
+    work.relay(2, attention_set)
+    work.relays(3, attention_set)
+    work.start_early([3])
+    work.ready([4])
+    work.start_own([4])
+    work.arrived(0)
+    load = pltpu.make_async_copy(gains_all, gain_tiles, load_sems.at[0])
+    load.start()
+    load.wait()
+    features = width // (4 * zn)
+    for owner in range(4 * zn):
+        for i in range(2):
+            gain_rows[pl.ds(i, 1), pl.ds(owner * features, features)] = gain_tiles[
+                pl.ds(owner * 8 + i, 1), :features
+            ]
+    save_gains = pltpu.make_async_copy(gain_rows, gain_out, load_sems.at[1])
+    save_gains.start()
+    gain_one, gain = gain_rows[pl.ds(0, 1)], gain_rows[pl.ds(1, 1)]
+    for copies in shared:
+        for copy in copies:
+            copy.wait()
+    work.arrived(1)
+    work.arrived(2)
+    save_gains.wait()
     half = total_refs[1]
 
     def attention(qkv, o, inputs, normed_one, turned, context, attended):
@@ -883,7 +919,12 @@
             return pl.ds(pl.multiple_of(place_of(i) * block, block), block)
 
         def fetch_inputs(i, slot):
-            return pltpu.make_async_copy(chip_tokens.at[rows_at(i)], inputs.at[slot], grad_sems.at[slot])
+            which = place_of(i)
+            return pltpu.make_async_copy(
+                chip_tokens.at[which // per, pl.ds(pl.multiple_of(lax.rem(which, per) * block, block), block)],
+                inputs.at[slot],
+                grad_sems.at[slot],
+            )
 
         def stores(i, slot):
             return [
@@ -927,7 +968,7 @@
             def norm(at):
                 value = inputs[slot, at].astype(F32)
                 factor = lax.rsqrt(jnp.mean(value * value, axis=-1, keepdims=True) + norm_eps)
-                normed_one[slot, at] = (value * factor * gain_one[...]).astype(BF16)
+                normed_one[slot, at] = (value * factor * gain_one).astype(BF16)
 
             by_rows(block, norm)
             cosine, sine = cosines[to], sines[to]
@@ -941,9 +982,8 @@
                 is_key, value * cosine + partner(value) * sine, value
             ).astype(BF16)
             which = place_of(i)
-            attention_block(
-                turned.at[slot], context.at[slot], queries_wide, columns_of[which], rows_of[which]
-            )
+            row = seg_pair[which // per, pl.ds(lax.rem(which, per), 1)]
+            attention_block(turned.at[slot], context.at[slot], queries_wide, row)
             for copy in stores(i, slot):
                 copy.start()
             return slot
@@ -963,15 +1003,15 @@
         for i in range(per):
             store_term(i, i % 2).wait()
         total.core().start()
-        work.start_early(range(3))
+        work.relay(1, [3])
+        work.relay(2, [3])
+        work.relay(1, [5])
+        work.relay(2, [5])
         loop(per, own)
         for i in range(blocks - 2, blocks):
             for copy in stores(i, i % 2):
                 copy.wait()
 
-    work.start()
-    work.ready(range(3))
-    work.start_own([0, 1])
     pl.run_scoped(
         attention,
         pltpu.VMEM(qkv_all.shape, BF16),
@@ -983,8 +1023,10 @@
         pltpu.VMEM((2, block, width), BF16),
     )
     total.meet(False)
-    work.relay(1, [0, 1])
-    work.start_own([2])
+    work.start_early([4])
+    work.relays(3, [3])
+    work.relay(1, [4])
+    work.relay(2, [4])
 
     def sums(mid):
         total.pair().wait_recv()
@@ -993,7 +1035,7 @@
             value = tokens[at].astype(F32) + total.rows(at)
             mid[at] = value
             factor = lax.rsqrt(jnp.mean(value * value, axis=-1, keepdims=True) + norm_eps)
-            normed[c, at] = (value * factor * gain[...]).astype(BF16)
+            normed[c, at] = (value * factor * gain).astype(BF16)
 
         by_rows(count, body)
         save = pltpu.make_async_copy(mid, mid_out, out_sems.at[0])
@@ -1002,17 +1044,19 @@
             copy.start()
         save.wait()
 
-    def hidden(first, second, silu, slope, up_grad, grads, result, stages, back_stage):
+    def hidden(first, second, silu, slope, up_grad, inputs, result, stages, back_stage):
         def fetch_grads(i, slot):
             return pltpu.make_async_copy(
-                chip_grads.at[pl.ds(pl.multiple_of(i * block, block), block)], grads.at[slot], grad_sems.at[slot]
+                chip_grads.at[i // per, pl.ds(pl.multiple_of(lax.rem(i, per) * block, block), block)],
+                inputs.at[slot],
+                grad_sems.at[slot],
             )
 
         def at_block(i):
             return pl.ds(pl.multiple_of(i * block, block), block)
 
         fetch_grads(0, 0).start()
-        work.arrived(0)
+        work.arrived(3)
         load = pltpu.make_async_copy(down_all, first, load_sems.at[0])
         load.start()
         load.wait()
@@ -1025,10 +1069,13 @@
             def _():
                 fetch_grads(i + 1, 1 - slot).start()
 
-            slope[at_block(i)] = product(grads[slot], first[...])
+            slope[at_block(i)] = product(inputs[slot], first[...])
 
         loop(blocks, hidden_block)
-        work.arrived(1)
+        work.relays(3, [4])
+        pl.run_scoped(sums, pltpu.VMEM((count, width), F32))
+        work.relays(3, [5])
+        work.arrived(4)
         load = pltpu.make_async_copy(gate_all, second, load_sems.at[1])
         load.start()
         share(here, normed.at[c], normed, pair_sems)[1].wait()
@@ -1053,8 +1100,7 @@
         loop(blocks, gate_block)
         save_up = pltpu.make_async_copy(up_grad, up_grad_out, out_sems.at[2])
         save_up.start()
-        work.relays(3, [2])
-        work.arrived(2)
+        work.arrived(5)
         load = pltpu.make_async_copy(up_all, first, load_sems.at[0])
         load.start()
         load.wait()
@@ -1100,11 +1146,6 @@
         save.wait()
         save_up.wait()
 
-    work.relay(2, [0, 1])
-    work.relay(1, [2])
-    pl.run_scoped(sums, pltpu.VMEM((count, width), F32))
-    work.relays(3, [0, 1])
-    work.relay(2, [2])
     pl.run_scoped(
         hidden,
         pltpu.VMEM((width, columns), BF16),
@@ -1119,6 +1160,8 @@
     )
     work.finish()
     total.finish()
+    for copy in saves:
+        copy.wait()
 
 
 def fetch(pairs, sems):
@@ -1130,10 +1173,10 @@
 
 def scatter_feedforward(zn, early, *refs):
     normed, gate_grad, chip_grads, activated, back_term, down_all, mid_in, gain = refs[:8]
-    turned_all, o_all, qkv_all, cosines, sines, columns_of, rows_of = refs[8:15]
-    gate_out, down_out, out, mid_grad_out, branch_out, gain_out, qkv_back, in_term = refs[15:23]
-    gate, down, out_term = refs[23:26]
-    buffers, refs = refs[26 : 26 + 2 * SCATTER_BUFFERS], refs[26 + 2 * SCATTER_BUFFERS :]
+    turned_all, o_all, qkv_all, cosines, sines, rows_of = refs[8:14]
+    gate_out, down_out, out, mid_grad_out, branch_out, gain_out, qkv_back, in_term = refs[14:22]
+    gate, down, out_term = refs[22:25]
+    buffers, refs = refs[25 : 25 + 2 * SCATTER_BUFFERS], refs[25 + 2 * SCATTER_BUFFERS :]
     back_refs, out_refs = refs[:4], refs[4:8]
     fetch_sems, out_sems, pair_sems, weight_sems, stage_sems, block_sems, back_sems = refs[8:15]
     branch, out_rows = back_refs[0], out_refs[0]
@@ -1341,7 +1384,6 @@
                 backs.at[slot],
                 accumulators,
                 queries_wide,
-                columns_of[i],
                 rows_of[i],
                 cosine[slot],
                 sine[slot],
@@ -1575,12 +1617,47 @@
     gain_rows = gain_rows.at[0, :rows].set(attn_gain.astype(F32)).at[1, :rows].set(mlp_gain.astype(F32))
     gain_shard = jnp.stack([gain_rows, gain_rows])
 
-    qkv_full, o_full, gains, tokens_two, grads_two, seg_two = call(
-        functools.partial(gather_attention, zn, early),
-        "gather_attention",
+    chip = 2 * count
+    inverse = 1.0 / 10000.0 ** (jnp.arange(0, HEAD_DIM, 2, dtype=F32) / HEAD_DIM)
+    inverse = jnp.tile(inverse, 4).reshape(1, 2 * HEAD_DIM)
+    sign = jnp.tile(jnp.repeat(jnp.array([-1.0, 1.0], F32), HEAD_DIM // 2), 2).reshape(1, 2 * HEAD_DIM)
+    (
+        qkv_full,
+        o_full,
+        grads_chip,
+        segment,
+        down_full,
+        mid,
+        normed_two,
+        activated,
+        gate_grad,
+        up_grad,
+        back_term,
+        normed,
+        turned,
+        context,
+        cosines,
+        sines,
+        gain_rows,
+    ) = call(
+        functools.partial(forward, zn, early),
+        "forward",
         0,
-        (q_weight, kv_shard, o_weight.T, gain_shard, tokens, out_grad, seg_ids),
-        [VMEM] * 7,
+        (
+            q_weight,
+            kv_shard,
+            o_weight.T,
+            gain_shard,
+            tokens,
+            out_grad,
+            seg_ids,
+            gate_weight,
+            up_weight,
+            down_weight.T,
+            inverse,
+            sign,
+        ),
+        [VMEM] * 12,
         [
             ((width, qkv_half), BF16),
             ((width, q_half), BF16),
@@ -1588,57 +1665,38 @@
             ((2, count, width), BF16),
             ((2, count, width), BF16),
             ((2,) + seg_ids.shape, jnp.int32),
-        ],
-        [ANY] * 6,
-        [DMA((3,))] * 3 + gather_sems(3, 4, zn),
-    )
-    gains = gains.reshape(dp, 8, 128)[:, :, :rows]
-    gain_one, gain_two = gains[:, 0].reshape(1, width), gains[:, 1].reshape(1, width)
-    chip = 2 * count
-    tokens_chip = tokens_two.reshape(chip, width)
-    grads_chip = grads_two.reshape(chip, width)
-    segment = seg_two.reshape(blocks, block_rows)
-
-    order = jnp.arange(block_rows, dtype=jnp.int32)
-    same = segment[:, :, None] == segment[:, None, :]
-    position = jnp.sum((same & (order[None, :] < order[:, None])).astype(jnp.int32), axis=2)
-    inverse = 1.0 / 10000.0 ** (jnp.arange(0, HEAD_DIM, 2, dtype=F32) / HEAD_DIM)
-    angles = position.astype(F32).reshape(chip, 1) * jnp.tile(inverse, 4)
-    sign = jnp.tile(jnp.repeat(jnp.array([-1.0, 1.0], F32), HEAD_DIM // 2), 2)
-    cosines, sines = jnp.cos(angles), jnp.sin(angles) * sign
-
-    mid, normed_two, activated, gate_grad, up_grad, back_term, down_full, normed, turned, context = call(
-        functools.partial(feedforward, zn, early),
-        "feedforward",
-        1,
-        (
-            gate_weight,
-            up_weight,
-            down_weight.T,
-            tokens,
-            gain_two,
-            grads_chip,
-            tokens_chip,
-            gain_one,
-            qkv_full,
-            o_full,
-            cosines,
-            sines,
-            segment[:, :, None],
-            segment[:, None, :],
-        ),
-        [VMEM] * 5 + [ANY] * 2 + [VMEM] + [ANY] * 2 + [VMEM] * 4,
-        [((width, ff_half), BF16)] * 3
+        ]
+        + [((width, ff_half), BF16)] * 3
         + [((count, width), F32), ((2, count, width), BF16)]
         + [((chip, ff_half), BF16)] * 3
         + [((2, count, width), BF16)] * 2
-        + [((chip, width), BF16), ((chip, qkv_half), BF16), ((chip, q_half), BF16)],
-        [ANY] * 13,
+        + [((chip, width), BF16), ((chip, qkv_half), BF16), ((chip, q_half), BF16)]
+        + [((chip, 2 * HEAD_DIM), F32)] * 2
+        + [((8, width), F32)],
+        [ANY] * 22,
         total_buffers(count, width)
-        + [pltpu.VMEM((2, count, width), BF16), DMA((3,)), DMA((3,)), DMA((2,)), DMA((2,)), DMA((2, 3)), DMA((2,))]
-        + gather_sems(3, 3, zn),
-        order=(3, 4, 5, 6, 7, 8, 2, 10, 11, 12),
-    )
+        + [
+            pltpu.VMEM((2, count, width), BF16),
+            DMA((3,)),
+            DMA((3,)),
+            DMA((2,)),
+            DMA((2,)),
+            DMA((2, 3)),
+            DMA((2,)),
+            pltpu.VMEM((chip, 2 * HEAD_DIM), F32),
+            pltpu.VMEM((chip, 2 * HEAD_DIM), F32),
+            pltpu.VMEM((2,) + seg_ids.shape, jnp.int32),
+            pltpu.VMEM((units * 16, 128), F32),
+            pltpu.VMEM((8, width), F32),
+            DMA((2, 3)),
+            DMA((5,)),
+        ]
+        + gather_sems(6, 7, zn),
+        order=(0, 1, 4, 5, 8, 9, 10, 11, 12, 13, 14, 16, 17, 18, 19, 20, 21),
+    )
+    gain_one, gain_two = gain_rows[0:1], gain_rows[1:2]
+    grads_chip = grads_chip.reshape(chip, width)
+    segment = segment.reshape(blocks, 1, block_rows)
     normed_two = normed_two.reshape(chip, width)
 
     gate_sum, down_sum, out, mid_grad, branch, gain_two_grad, qkv_back, in_term = call(
@@ -1659,10 +1717,9 @@
             qkv_full,
             cosines,
             sines,
-            segment[:, :, None],
-            segment[:, None, :],
+            segment,
         ),
-        [ANY] * 7 + [VMEM] + [ANY] * 5 + [VMEM] * 2,
+        [ANY] * 7 + [VMEM] + [ANY] * 5 + [VMEM],
         [((rows, 2 * ff_half), F32)] * 2
         + [
             ((count, width), BF16),

time: 583 us -> 557 us (0.955)
  Pallas kernels: 550 us -> 528 us
    pallas_call x4 -> x3, Pallas kernels: 550 us -> 528 us  [call(): pl.pallas_call(kernel, out_shape=[jax.ShapeDtypeStruct(shape, dtype) for...]
    unnamed x28 -> x23, local copies, waits for them, and re-layouts: 15.1 us -> 16.2 us
where the time goes in v1:
time: 557 us; the launch traced here: 555 us
  Pallas kernels  528 us (95%)
  local copies, waits for them, and re-layouts  23.6 us (4%)
    pallas_call x3, Pallas kernels, call(): pl.pallas_call(kernel, out_shape=[jax.ShapeDtypeStruct(shape, dtype) for...  528 us
    unnamed x23, local copies, waits for them, and re-layouts  16.2 us

profile of v1, /device:TPU:0, one launch (start us, length us, event | category | flops | bytes accessed | tf_op | source)
XLA Modules:
  0.0 555.5 jit_solution(6381666727565281312)
XLA Ops:
  0.6 2.2 copy.33
  2.9 1.8 copy.32
  4.7 0.9 copy.28
  5.5 0.1 copy.29
  5.7 0.9 copy.30
  6.5 0.1 copy.31
  6.7 0.7 pad_maximum_fusion.refs_1_
  7.4 0.7 bitcast_convert_fusion
  8.1 0.7 bitcast_convert_fusion.1
  8.8 0.6 pad_maximum_fusion.3.refs_3_
  9.4 0.6 reshape_tile.6.refs_10_
  10.0 0.7 broadcast_in_dim.4
  10.7 0.1 tile.14
  10.8 0.6 reshape_tile.7.refs_11_
  11.4 261.7 %forward.1 = (bf16[2048,640]{1,0:T(8,128)(2,1)}, bf16[2048,512]{1,0:T(8,128)(2,1)}, f32[128,128]{1,0:T(8,128)}, bf16[2,512,2048]{2,1,0:T(8,128)(2,1)}, bf16[2,51...) custom-call(bf16[128,1024]{1,0:T(8,128)(2,1)} %refs_0_.1, ...), custom_call_target="tpu_custom_call" | custom-call | tf_op jit(solution)/shard_map/forward/pallas_call | solution.py:1541
  273.1 1.5 fusion
  274.6 1.3 reshape.108.refs_13_
  275.9 135.8 %scatter_feedforward.1 = (f32[128,2816]{1,0:T(8,128)}, f32[128,2816]{1,0:T(8,128)}, bf16[512,2048]{1,0:T(8,128)(2,1)}, f32[512,2048]{1,0:T(8,128)}, bf16[2,512,2...) custom-call(bf16[1024,2048]{1,0:T(8,128)(2,1)} %bitcast.30, ...), custom_call_target="tpu_custom_call" | custom-call | tf_op jit(solution)/shard_map/scatter_feedforward/pallas_call | solution.py:1541
  411.7 0.0 copy-start.3
  411.7 130.2 %scatter_attention.1 = (f32[128,1024]{1,0:T(8,128)}, f32[2,128,128]{2,1,0:T(8,128)}, f32[128,1024]{1,0:T(8,128)}, f32[128,2816]{1,0:T(8,128)}, bf16[512,2048]{1,...) custom-call(bf16[1024,2048]{1,0:T(8,128)(2,1)} %get-tuple-element.81, ...), custom_call_target="tpu_custom_call" | custom-call | tf_op jit(solution)/shard_map/scatter_attention/pallas_call | solution.py:1541
  541.9 0.0 copy-start
  541.9 1.2 slice_bitcast_fusion.1
  543.1 0.8 pad_maximum_fusion.1
  543.9 2.0 copy.34
  545.9 0.7 constant_dynamic-slice_fusion
  546.6 0.5 slice_bitcast_fusion.4
  547.1 0.0 copy-done.3
  547.1 1.5 copy.35
  548.6 0.0 copy-start.1
  548.6 0.0 copy-done
  548.6 1.3 copy.42
  550.0 1.0 copy-done.1
  551.0 0.0 copy-start.5
  551.0 0.0 copy-start.2
  551.0 1.3 copy.43
  552.3 0.1 copy-done.5
  552.3 0.0 copy-start.4
  552.4 0.8 copy.44
  553.1 0.1 copy-done.2
  553.3 1.1 copy.45
  554.4 0.0 copy-done.4
  554.4 1.1 copy.46
  (4 shorter events, 0.0 us)
Async XLA Ops:
  411.7 135.4 %copy-start.3 = (f32[128,2816]{1,0:T(8,128)S(1)}, f32[128,2816]{1,0:T(8,128)}, u32[]{:S(2)}) copy-start(f32[128,2816]{1,0:T(8,128)} %get-tuple-element.96) | copy-start | bytes 4325380
  541.9 6.7 %copy-start = (bf16[512,2048]{1,0:T(8,128)(2,1)S(1)}, bf16[512,2048]{1,0:T(8,128)(2,1)}, u32[]{:S(2)}) copy-start(bf16[512,2048]{1,0:T(8,128)(2,1)} %get-tuple-element.140) | copy-start | bytes 6291460
  548.6 2.3 copy-start.1
  551.0 1.4 copy-start.5
  551.0 2.3 copy-start.2
  552.3 2.0 copy-start.4

commit v2 on v1

--- a/solution.py
+++ b/solution.py
@@ -424,7 +424,6 @@
         def both(i):
             compute(i)
             send(i - 1)
-            self.hop_early(j, i - 1)
 
         compute(0)
         if between is not None:
@@ -492,20 +491,16 @@
 
         self.along(j, o, slot, down).start()
 
-    def late_hops(self, j):
-        self.early_home(j)
-        loop(self.zn - 1, lambda i: self.hop(j, i))
-
-    def share_of_hops(self, j, i, shares):
+    def third(self, hop, j, g):
         hops = self.zn - 1
-        first = i * hops // (shares - 1)
-        last = jnp.minimum((i + 1) * hops // (shares - 1), hops)
-
-        def step(hop, carry):
-            self.hop(j, hop)
-            return carry
-
-        lax.fori_loop(first, last, step, 0)
+        first = g * hops // 3
+        loop((g + 1) * hops // 3 - first, lambda i: hop(j, first + i))
+
+    def early_third(self, j, g):
+        self.third(self.hop_early, j, g)
+
+    def late_third(self, j, g):
+        self.third(self.hop, j, g)
 
     def at_home(self, action):
         z, zn = self.here[2], self.zn
@@ -535,51 +530,72 @@
         self.at_home(home)
         self.across_early(j).start()
 
-    def finish(self):
-        z, zn = self.here[2], self.zn
-        n = len(self.term)
-        for j in range(n):
-            own, got, line, early, _, other_early, total = self.buffers[j]
-            late = self.late(j)
-            self.load(j, z).wait()
-            self.across(j, z).wait_recv()
-
-            def home(slots):
+    def home(self, j):
+        z = self.here[2]
+        own, got, line, early, _, other_early, total = self.buffers[j]
+        late = self.late(j)
+        self.load(j, z).wait()
+        self.across(j, z).wait_recv()
+
+        def last(slots):
+            for slot in slots:
+                self.along(j, z, slot, 0).wait_recv()
+
+            def body(at):
+                value = own[z, at].astype(F32) + got[z, at].astype(F32)
                 for slot in slots:
-                    self.along(j, z, slot, 0).wait_recv()
-
-                def body(at):
-                    value = own[z, at].astype(F32) + got[z, at].astype(F32)
-                    for slot in slots:
-                        value = value + line[slot, at].astype(F32)
-                    total[at] = value
-
-                by_rows(late, body)
-
-            self.at_home(home)
-            self.across_early(j).wait_recv()
-            for i in range(self.early // 16):
-                at = pl.ds(16 * i, 16)
-                total[pl.ds(late + 16 * i, 16)] = early[z, 0, at].astype(F32) + other_early[at].astype(F32)
-            for r, result in enumerate(self.results):
-                if result[0] == j:
-                    self.give(r).start()
-                    self.keep(r).start()
-        for r in range(len(self.results)):
-            self.give(r).wait()
-            self.keep(r).wait()
-        for j in range(n):
-            self.across_early(j).wait_send()
-
-            def sent(o, j=j):
-                self.across(j, o).wait_send()
-
-                @pl.when(o != z)
-                def _():
-                    self.along(j, o, 0, 0).wait_send()
-                    self.along_early(j, o, 0, 0).wait_send()
-
-            loop(zn, sent)
+                    value = value + line[slot, at].astype(F32)
+                total[at] = value
+
+            by_rows(late, body)
+
+        self.at_home(last)
+        self.across_early(j).wait_recv()
+        for i in range(self.early // 16):
+            at = pl.ds(16 * i, 16)
+            total[pl.ds(late + 16 * i, 16)] = early[z, 0, at].astype(F32) + other_early[at].astype(F32)
+        for r, result in enumerate(self.results):
+            if result[0] == j:
+                self.give(r).start()
+                self.keep(r).start()
+
+    def done(self, j):
+        z = self.here[2]
+        for r, result in enumerate(self.results):
+            if result[0] == j:
+                self.give(r).wait()
+                self.keep(r).wait()
+        self.across_early(j).wait_send()
+
+        def sent(o):
+            self.across(j, o).wait_send()
+
+            @pl.when(o != z)
+            def _():
+                self.along(j, o, 0, 0).wait_send()
+                self.along_early(j, o, 0, 0).wait_send()
+
+        loop(self.zn, sent)
+
+    def lend(self, credit):
+        d, t, z, x, c = self.here
+
+        def tell(device):
+            pl.semaphore_signal(credit, inc=1, device_id=device, device_id_type=MESH)
+
+        tell((d + 2 - 4 * x, t))
+
+        @pl.when(z > 0)
+        def _():
+            tell((d - 4, t))
+
+        @pl.when(z < self.zn - 1)
+        def _():
+            tell((d + 4, t))
+
+    def borrow(self, credit):
+        z = self.here[2]
+        pl.semaphore_wait(credit, 3 - (z == 0).astype(jnp.int32) - (z == self.zn - 1).astype(jnp.int32))
 
 
 class Gains:
@@ -588,7 +604,7 @@
 
     def swap(self, i):
         d, t, z, x, c = self.here
-        device = ((d + 1 - 2 * c, t), (d + 2 - 4 * x, t), (d, 1 - t))[i]
+        device = ((d + 1 - 2 * c, t), (d, 1 - t), (d + 2 - 4 * x, t))[i]
         return remote(self.own, self.got.at[i], self.sems.at[0, i], self.sems.at[1, i], device)
 
     def along(self, o, slot, down):
@@ -694,19 +710,17 @@
         d, t, z, x, c = self.here
         return remote(self.half, self.from_pair, self.sems.at[2], self.sems.at[3], (d, 1 - t))
 
-    def meet(self, loaded=True):
+    def meet(self, loaded=True, send=True):
         if loaded:
             self.load().wait()
         self.core().wait_recv()
-        block = 16
-
-        def body(i, carry):
-            at = pl.ds(pl.multiple_of(i * block, block), block)
+
+        def body(at):
             self.half[at] = (self.half[at].astype(F32) + self.from_core[at].astype(F32)).astype(BF16)
-            return carry
-
-        lax.fori_loop(0, self.half.shape[0] // block, body, 0)
-        self.pair().start()
+
+        by_rows(self.half.shape[0], body)
+        if send:
+            self.pair().start()
 
     def rows(self, at):
         return self.half[at].astype(F32) + self.from_pair[at].astype(F32)
@@ -1171,34 +1185,46 @@
     return copies
 
 
-def scatter_feedforward(zn, early, *refs):
-    normed, gate_grad, chip_grads, activated, back_term, down_all, mid_in, gain = refs[:8]
-    turned_all, o_all, qkv_all, cosines, sines, rows_of = refs[8:14]
-    gate_out, down_out, out, mid_grad_out, branch_out, gain_out, qkv_back, in_term = refs[14:22]
-    gate, down, out_term = refs[22:25]
-    buffers, refs = refs[25 : 25 + 2 * SCATTER_BUFFERS], refs[25 + 2 * SCATTER_BUFFERS :]
-    back_refs, out_refs = refs[:4], refs[4:8]
-    fetch_sems, out_sems, pair_sems, weight_sems, stage_sems, block_sems, back_sems = refs[8:15]
-    branch, out_rows = back_refs[0], out_refs[0]
+def backward(zn, early, *refs):
+    normed_two, gate_grad, chip_grads, activated, back_term, down_all, mid_in, up_grad, normed_one, context = refs[:10]
+    turned_all, o_all, qkv_all, cosines, sines, tokens_in, rows_of, gain_rows = refs[10:18]
+    down_out, gate_out, up_out, o_out, q_out, kv_out, out, in_grad, gain_out = refs[18:27]
+    mid_grad_all, branch_all, qkv_back, in_term, out_term, down, gate, up, o_sums, qkv_sums = refs[27:37]
+    n = SCATTER_BUFFERS
+    buffers, refs = refs[37 : 37 + 4 * n], refs[37 + 4 * n :]
+    back_refs, front_refs, in_refs = refs[:4], refs[4:8], refs[8:11]
+    gain_refs, (one_sum, two_sum), refs = refs[11:15], refs[15:17], refs[17:]
+    fetch_sems, out_sems, pair_sems, weight_sems, stage_sems, block_sems, back_sems, credit = refs[:8]
     here = place()
-    c = here[4]
+    z, c = here[2], here[4]
     chip, width = chip_grads.shape
+    count = chip // 2
+    block = rows_of.shape[2]
+    blocks = chip // block
+    per = blocks // 2
+    qkv_wide, q_half = qkv_all.shape[1], o_all.shape[1]
     enter(zn, here)
+    branch, out_rows, in_rows = back_refs[0], front_refs[0], in_refs[0]
     back = Total(here, back_term, *back_refs)
-    front = Total(here, out_term, *out_refs)
+    front = Total(here, out_term, *front_refs)
+    total = Total(here, in_term, in_refs[0], back_refs[1], in_refs[1], in_refs[2])
+    gains = Gains(zn, here, *gain_refs)
     work = Scatter(
         zn,
         here,
         early,
         [
+            (down, buffers[:n], [(down_out, False, 0, down_out.shape[1] // 2)]),
+            (gate, buffers[n : 2 * n], [(gate_out, False, 0, gate_out.shape[1] // 2)]),
+            (up, buffers[:n], [(up_out, False, 0, up_out.shape[1] // 2)]),
+            (o_sums, buffers[2 * n : 3 * n], [(o_out, False, 0, q_half)]),
             (
-                term,
-                buffers[SCATTER_BUFFERS * j : SCATTER_BUFFERS * (j + 1)],
-                [(result, False, 0, result.shape[1] // 2)],
-            )
-            for j, (term, result) in enumerate(((down, down_out), (gate, gate_out)))
+                qkv_sums,
+                buffers[3 * n :],
+                [(q_out, False, 0, q_half), (kv_out, True, q_half, kv_out.shape[2])],
+            ),
         ],
-        refs[15:],
+        refs[8:],
     )
     back.start()
 
@@ -1245,62 +1271,57 @@
             for copy in stores(i, i % 2):
                 copy.wait()
 
-    def terms(left_one, right_one, left_two, right_two, stage, weights, stages):
-        copies = fetch(
+    def first_terms(left, right, stage, weights, stages):
+        for load in fetch(((chip_grads, left), (activated, right)), fetch_sems):
+            load.wait()
+        work.make(0, left, right, stage, back.meet)
+        load = fetch(((normed_two, left),), fetch_sems)[0]
+        for g in range(3):
+            work.early_third(0, g)
+        work.late_third(0, 0)
+        out_terms(right, weights, stages)
+        front.start()
+        load_right = pltpu.make_async_copy(gate_grad, right, fetch_sems.at[1])
+        load_right.start()
+        work.early_home(0)
+        work.late_third(0, 1)
+        work.late_third(0, 2)
+        load.wait()
+        load_right.wait()
+        work.make(1, left, right, stage)
+
+    wide = down.shape[2]
+    operands = [pltpu.VMEM((chip, width), BF16), pltpu.VMEM((chip, wide), BF16), pltpu.VMEM((2,) + down.shape[1:], BF16)]
+    pl.run_scoped(
+        first_terms, *operands, pltpu.VMEM((2, 256, wide), BF16), pltpu.VMEM((2, chip, 256), BF16)
+    )
+    work.early_third(1, 0)
+    work.early_third(1, 1)
+
+    def sums(mid, mid_grad, grads):
+        for load in fetch(
             (
-                (chip_grads, left_one),
-                (activated, right_one),
-                (normed, left_two),
-                (gate_grad, right_two),
+                (mid_in, mid),
+                (chip_grads.at[pl.ds(pl.multiple_of(c * count, 16), count)], grads),
             ),
             fetch_sems,
-        )
-        copies[0].wait()
-        copies[1].wait()
-        work.make(0, left_one, right_one, stage, back.meet)
-        copies[2].wait()
-        copies[3].wait()
-        work.make(1, left_two, right_two, stage)
-        out_terms(right_one, weights, stages)
-        front.start()
-
-    pl.run_scoped(
-        terms,
-        pltpu.VMEM(chip_grads.shape, BF16),
-        pltpu.VMEM(activated.shape, BF16),
-        pltpu.VMEM(normed.shape, BF16),
-        pltpu.VMEM(gate_grad.shape, BF16),
-        pltpu.VMEM((2,) + down.shape[1:], BF16),
-        pltpu.VMEM((2, 256, down.shape[2]), BF16),
-        pltpu.VMEM((2, chip, 256), BF16),
-    )
-
-    def sums(mid, mid_grad, grads):
-        copies = fetch(
-            (
-                (mid_in, mid),
-                (chip_grads.at[pl.ds(pl.multiple_of(c * (chip // 2), 16), chip // 2)], grads),
-            ),
-            fetch_sems,
-        )
-        work.late_hops(0)
-        front.meet()
-        for copy in copies:
-            copy.wait()
-        gain_out[...] = jnp.zeros_like(gain_out)
+        ):
+            load.wait()
+        gain = gain_rows[pl.ds(1, 1)]
+        two_sum[...] = jnp.zeros_like(two_sum)
 
         def body_gain(at):
             value = mid[at]
             factor = lax.rsqrt(jnp.mean(value * value, axis=-1, keepdims=True) + norm_eps)
-            gain_out[...] += jnp.sum(back.half[at].astype(F32) * (value * factor), axis=0, keepdims=True)
-
-        by_rows(chip // 2, body_gain)
+            two_sum[...] += jnp.sum(back.half[at].astype(F32) * (value * factor), axis=0, keepdims=True)
+
+        by_rows(count, body_gain)
         back.pair().wait_recv()
 
         def body(at):
             value = mid[at]
             factor = lax.rsqrt(jnp.mean(value * value, axis=-1, keepdims=True) + norm_eps)
-            scaled = back.rows(at) * gain[...]
+            scaled = back.rows(at) * gain
             result = (
                 grads[at].astype(F32)
                 + factor * scaled
@@ -1309,53 +1330,77 @@
             mid_grad[at] = result
             branch[at] = result.astype(BF16)
 
-        by_rows(chip // 2, body)
-        save = pltpu.make_async_copy(mid_grad, mid_grad_out, out_sems.at[0])
+        by_rows(count, body)
+        save = pltpu.make_async_copy(mid_grad, mid_grad_all, out_sems.at[0])
         save.start()
-        for copy in share(here, branch, branch_out, pair_sems):
+        for copy in share(here, branch, branch_all, pair_sems):
             copy.start()
-        work.early_home(1)
+        work.early_third(1, 2)
         save.wait()
 
     pl.run_scoped(
-        sums,
-        pltpu.VMEM((chip // 2, width), F32),
-        pltpu.VMEM((chip // 2, width), F32),
-        pltpu.VMEM((chip // 2, width), BF16),
+        sums, pltpu.VMEM((count, width), F32), pltpu.VMEM((count, width), F32), pltpu.VMEM((count, width), BF16)
     )
+    work.home(0)
+    work.late_third(1, 0)
+    work.done(0)
+    work.lend(credit)
+
+    def middle_terms(left, right, stage):
+        for copy in share(here, branch, branch_all, pair_sems):
+            copy.wait()
+        right_o = right.at[:, pl.ds(0, q_half)]
+        loads = fetch(
+            ((branch_all.at[0], left.at[pl.ds(0, count)]), (branch_all.at[1], left.at[pl.ds(count, count)])),
+            fetch_sems,
+        )
+        loads.append(pltpu.make_async_copy(context, right_o, fetch_sems.at[2]))
+        loads[2].start()
+        for load in loads:
+            load.wait()
+        work.make(3, left, right_o, stage)
+        loads = fetch(((normed_two, left), (up_grad, right)), fetch_sems)
+        front.meet()
+        work.late_third(1, 1)
+        for load in loads:
+            load.wait()
+        work.borrow(credit)
+        work.make(2, left, right, stage)
+
+    pl.run_scoped(middle_terms, *operands)
+    work.early_third(2, 0)
+    work.late_third(1, 2)
 
     def attention(o, qkv, inputs, turned, grads, backs, terms_out, cosine, sine, accumulators):
-        block = inputs.shape[1]
-        blocks = chip // block
-        per = blocks // 2
-        queries_wide = o.shape[1]
+        def which(i):
+            return lax.rem((1 - c) * per + i, blocks)
 
         def rows_at(i):
             return pl.ds(pl.multiple_of(i * block, block), block)
 
         def fetches(i, slot):
+            b = which(i)
             sources = (
-                (branch_out.at[i // per, rows_at(lax.rem(i, per))], inputs),
-                (turned_all.at[rows_at(i)], turned),
-                (cosines.at[rows_at(i)], cosine),
-                (sines.at[rows_at(i)], sine),
+                (branch_all.at[b // per, rows_at(lax.rem(b, per))], inputs),
+                (turned_all.at[rows_at(b)], turned),
+                (cosines.at[rows_at(b)], cosine),
+                (sines.at[rows_at(b)], sine),
             )
             return [
-                pltpu.make_async_copy(source, buffer.at[slot], block_sems.at[slot, n])
-                for n, (source, buffer) in enumerate(sources)
+                pltpu.make_async_copy(source, buffer.at[slot], block_sems.at[slot, k])
+                for k, (source, buffer) in enumerate(sources)
             ]
 
         def stores(i, slot):
+            b = which(i)
             return [
-                pltpu.make_async_copy(backs.at[slot], qkv_back.at[rows_at(i)], back_sems.at[slot, 0]),
+                pltpu.make_async_copy(backs.at[slot], qkv_back.at[rows_at(b)], back_sems.at[slot, 0]),
                 pltpu.make_async_copy(
-                    terms_out.at[slot], in_term.at[i // per, rows_at(lax.rem(i, per))], back_sems.at[slot, 1]
+                    terms_out.at[slot], in_term.at[b // per, rows_at(lax.rem(b, per))], back_sems.at[slot, 1]
                 ),
             ]
 
         loads = fetch(((o_all, o), (qkv_all, qkv)), fetch_sems)
-        for copy in share(here, branch, branch_out, pair_sems):
-            copy.wait()
         for copy in fetches(0, 0):
             copy.start()
         for load in loads:
@@ -1363,7 +1408,23 @@
 
         def step(i):
             slot = lax.rem(i, 2)
-            work.share_of_hops(1, i, blocks)
+
+            @pl.when(i == per)
+            def _():
+                for done in range(per):
+                    for copy in stores(done, done % 2):
+                        copy.wait()
+                total.core().start()
+                work.early_home(1)
+                work.early_third(3, 0)
+                work.late_third(3, 0)
+                work.early_third(2, 1)
+
+            @pl.when(i == blocks - 1)
+            def _():
+                work.early_third(2, 2)
+                work.early_third(3, 1)
+
             for copy in fetches(i, slot):
                 copy.wait()
 
@@ -1371,11 +1432,6 @@
             def _():
                 for copy in fetches(i + 1, 1 - slot):
                     copy.start()
-
-            @pl.when(i > 1)
-            def _():
-                for copy in stores(i - 2, slot):
-                    copy.wait()
 
             grads[...] = product(inputs[slot], o[...]).astype(BF16)
             attention_block_back(
@@ -1383,8 +1439,8 @@
                 grads,
                 backs.at[slot],
                 accumulators,
-                queries_wide,
-                rows_of[i],
+                q_half,
+                rows_of[which(i)],
                 cosine[slot],
                 sine[slot],
             )
@@ -1393,25 +1449,60 @@
                 copy.start()
 
         loop(blocks, step)
-        for i in range(blocks - 2, blocks):
+        for i in range(per, blocks):
             for copy in stores(i, i % 2):
                 copy.wait()
 
-    block = rows_of.shape[2]
-    qkv_wide = qkv_all.shape[1]
     pl.run_scoped(
         attention,
         pltpu.VMEM(o_all.shape, BF16),
         pltpu.VMEM(qkv_all.shape, BF16),
         pltpu.VMEM((2, block, width), BF16),
         pltpu.VMEM((2, block, qkv_wide), BF16),
-        pltpu.VMEM((block, o_all.shape[1]), BF16),
+        pltpu.VMEM((block, q_half), BF16),
         pltpu.VMEM((2, block, qkv_wide), BF16),
         pltpu.VMEM((2, block, width), BF16),
         pltpu.VMEM((2, block, 2 * HEAD_DIM), F32),
         pltpu.VMEM((2, block, 2 * HEAD_DIM), F32),
         pltpu.VMEM((4, block, 2 * HEAD_DIM), F32),
     )
+    back.finish()
+    total.load().start()
+
+    def meeting(tokens):
+        load = fetch(((tokens_in, tokens),), fetch_sems)[0]
+        work.late_third(3, 1)
+        total.meet(send=False)
+        load.wait()
+        one_sum[...] = jnp.zeros_like(one_sum)
+
+        def body_gain(at):
+            value = tokens[at].astype(F32)
+            factor = lax.rsqrt(jnp.mean(value * value, axis=-1, keepdims=True) + norm_eps)
+            one_sum[...] += jnp.sum(total.half[at].astype(F32) * (value * factor), axis=0, keepdims=True)
+
+        by_rows(count, body_gain)
+
+    pl.run_scoped(meeting, pltpu.VMEM((count, width), BF16))
+    gains.start([one_sum, two_sum])
+    gains.swapped(0)
+    total.pair().start()
+    work.late_third(3, 2)
+    work.late_third(2, 0)
+
+    def last_terms(left, right, stage):
+        right_qkv = right.at[:, pl.ds(0, qkv_wide)]
+        for load in fetch(((normed_one, left), (qkv_back, right_qkv)), fetch_sems):
+            load.wait()
+        gains.swapped(1)
+        work.make(4, left, right_qkv, stage)
+
+    pl.run_scoped(last_terms, *operands)
+    work.early_third(4, 0)
+    work.early_third(4, 1)
+    work.late_third(2, 1)
+    work.early_third(3, 2)
+    work.late_third(2, 2)
 
     def output(mid):
         load = fetch(((mid_in, mid),), fetch_sems)[0]
@@ -1421,120 +1512,53 @@
         def body_out(at):
             out_rows[at] = (mid[at] + front.rows(at)).astype(BF16)
 
-        by_rows(chip // 2, body_out)
-
-    pl.run_scoped(output, pltpu.VMEM((chip // 2, width), F32))
+        by_rows(count, body_out)
+
+    pl.run_scoped(output, pltpu.VMEM((count, width), F32))
     save_out = pltpu.make_async_copy(out_rows, out, out_sems.at[1])
     save_out.start()
-    work.finish()
-    back.finish()
-    front.finish()
-    save_out.wait()
-
-
-def scatter_attention(zn, early, *refs):
-    normed, qkv_grad, branch, context, normed_two, up_grad, term, mid_grad_in, tokens, gain, two_sum = refs[:11]
-    q_out, kv_out, o_out, up_out, in_grad, gain_out, qkv, o, up = refs[11:20]
-    buffers, refs = refs[20 : 20 + 3 * SCATTER_BUFFERS], refs[20 + 3 * SCATTER_BUFFERS :]
-    total_refs, gain_refs = refs[:4], refs[4:8]
-    fetch_sems, out_sems, one_sum = refs[8:11]
-    rows_out = total_refs[0]
-    here = place()
-    enter(zn, here)
-    total = Total(here, term, *total_refs)
-    q_half = q_out.shape[1] // 2
-    work = Scatter(
-        zn,
-        here,
-        early,
-        [
-            (up, buffers[:SCATTER_BUFFERS], [(up_out, False, 0, up_out.shape[1] // 2)]),
-            (o, buffers[SCATTER_BUFFERS : 2 * SCATTER_BUFFERS], [(o_out, False, 0, o_out.shape[1] // 2)]),
-            (
-                qkv,
-                buffers[2 * SCATTER_BUFFERS :],
-                [(q_out, False, 0, q_half), (kv_out, True, q_half, kv_out.shape[2])],
-            ),
-        ],
-        refs[11:],
-    )
-    gains = Gains(zn, here, *gain_refs)
-    total.start()
-
-    def terms(left_one, right_one, left_two, right_two, right_three, stage):
-        copies = fetch(
-            (
-                (normed_two, left_one),
-                (up_grad, right_one),
-                (branch, left_two),
-                (context, right_two),
-                (qkv_grad, right_three),
-            ),
-            fetch_sems,
-        )
-        copies[0].wait()
-        copies[1].wait()
-        work.make(0, left_one, right_one, stage, total.meet)
-        last = pltpu.make_async_copy(normed, left_one, fetch_sems.at[5])
-        last.start()
-        one_sum[...] = jnp.zeros_like(one_sum)
-
-        def body_gain(at):
-            value = tokens[at].astype(F32)
-            factor = lax.rsqrt(jnp.mean(value * value, axis=-1, keepdims=True) + norm_eps)
-            one_sum[...] += jnp.sum(total.half[at].astype(F32) * (value * factor), axis=0, keepdims=True)
-
-        by_rows(tokens.shape[0], body_gain)
-        gains.start([one_sum, two_sum])
-        gains.swapped(0)
-        copies[2].wait()
-        copies[3].wait()
-        work.make(1, left_two, right_two, stage)
-        copies[4].wait()
-        last.wait()
-        work.make(2, left_one, right_three, stage)
-
-    pl.run_scoped(
-        terms,
-        pltpu.VMEM(normed.shape, BF16),
-        pltpu.VMEM(up_grad.shape, BF16),
-        pltpu.VMEM(branch.shape, BF16),
-        pltpu.VMEM(context.shape, BF16),
-        pltpu.VMEM(qkv_grad.shape, BF16),
-        pltpu.VMEM((2,) + up.shape[1:], BF16),
-    )
-
-    def sums(mid_grad):
-        copies = fetch(((mid_grad_in, mid_grad),), fetch_sems)
-        work.late_hops(0)
-        gains.swapped(1)
-        work.late_hops(1)
-        gains.swapped(2)
-        gains.run()
-        work.late_hops(2)
-        gains.finish(gain_out)
-        for copy in copies:
-            copy.wait()
+    work.home(1)
+    work.early_home(2)
+    work.early_home(3)
+    work.early_third(4, 2)
+    work.late_third(4, 0)
+    gains.swapped(2)
+    gains.run()
+
+    def inputs_back(mid_grad, tokens):
+        loads = fetch(((mid_grad_all, mid_grad), (tokens_in, tokens)), fetch_sems)
+        gain = gain_rows[pl.ds(0, 1)]
         total.pair().wait_recv()
+        for load in loads:
+            load.wait()
 
         def body(at):
             value = tokens[at].astype(F32)
             factor = lax.rsqrt(jnp.mean(value * value, axis=-1, keepdims=True) + norm_eps)
-            scaled = total.rows(at) * gain[...]
-            rows_out[at] = (
+            scaled = total.rows(at) * gain
+            in_rows[at] = (
                 mid_grad[at]
                 + factor * scaled
                 - value * (factor * factor * factor) * jnp.mean(scaled * value, axis=-1, keepdims=True)
             ).astype(BF16)
 
-        by_rows(tokens.shape[0], body)
-        save = pltpu.make_async_copy(rows_out, in_grad, out_sems.at[0])
-        save.start()
-        save.wait()
-
-    pl.run_scoped(sums, pltpu.VMEM(mid_grad_in.shape, F32))
-    work.finish()
+        by_rows(count, body)
+
+    pl.run_scoped(inputs_back, pltpu.VMEM((count, width), F32), pltpu.VMEM((count, width), BF16))
+    save_in = pltpu.make_async_copy(in_rows, in_grad, out_sems.at[0])
+    save_in.start()
+    work.late_third(4, 1)
+    work.late_third(4, 2)
+    work.early_home(4)
+    gains.finish(gain_out)
+    for j in (2, 3, 4):
+        work.home(j)
+    for j in (1, 2, 3, 4):
+        work.done(j)
+    front.finish()
     total.finish()
+    save_out.wait()
+    save_in.wait()
 
 
 def call(kernel, name, collective_id, operands, specs, outs, out_specs, scratch, order=None):
@@ -1546,7 +1570,7 @@
         scratch_shapes=scratch,
         name=name,
         compiler_params=pltpu.CompilerParams(
-            collective_id=collective_id, has_side_effects=True, vmem_limit_bytes=58 << 20
+            collective_id=collective_id, has_side_effects=True, vmem_limit_bytes=63 << 20
         ),
     )(*operands)
     return results if order is None else [results[i] for i in order]
@@ -1694,15 +1718,14 @@
         + gather_sems(6, 7, zn),
         order=(0, 1, 4, 5, 8, 9, 10, 11, 12, 13, 14, 16, 17, 18, 19, 20, 21),
     )
-    gain_one, gain_two = gain_rows[0:1], gain_rows[1:2]
     grads_chip = grads_chip.reshape(chip, width)
     segment = segment.reshape(blocks, 1, block_rows)
     normed_two = normed_two.reshape(chip, width)
 
-    gate_sum, down_sum, out, mid_grad, branch, gain_two_grad, qkv_back, in_term = call(
-        functools.partial(scatter_feedforward, zn, early_sums),
-        "scatter_feedforward",
-        2,
+    down_sum, gate_sum, up_sum, o_sum, q_sum, kv_sum, out, in_grad, gain_sums = call(
+        functools.partial(backward, zn, early_sums),
+        "backward",
+        1,
         (
             normed_two,
             gate_grad,
@@ -1711,71 +1734,56 @@
             back_term,
             down_full,
             mid,
-            gain_two,
+            up_grad,
+            normed,
+            context,
             turned,
             o_full,
             qkv_full,
             cosines,
             sines,
+            tokens,
             segment,
+            gain_rows,
         ),
-        [ANY] * 7 + [VMEM] + [ANY] * 5 + [VMEM],
-        [((rows, 2 * ff_half), F32)] * 2
+        [ANY] * 16 + [VMEM] * 2,
+        [((rows, 2 * ff_half), F32)] * 3
         + [
+            ((rows, 2 * q_half), F32),
+            ((rows, 2 * q_half), F32),
+            ((2, rows, 2 * kv_half), F32),
             ((count, width), BF16),
+            ((count, width), BF16),
+            ((8, 4 * rows), F32),
             ((count, width), F32),
             ((2, count, width), BF16),
-            ((1, width), F32),
             ((chip, qkv_half), BF16),
             ((2, count, width), BF16),
+            ((2, count, width), BF16),
         ]
-        + [((zn, 4 * rows, ff_half), BF16)] * 2
-        + [((2, count, width), BF16)],
-        [ANY] * 5 + [VMEM] + [ANY] * 5,
-        scatter_buffers([(2 * rows, ff_half)] * 2, early_sums, zn)
+        + [((zn, 4 * rows, ff_half), BF16)] * 3
+        + [((zn, 4 * rows, q_half), BF16), ((zn, 4 * rows, qkv_half), BF16)],
+        [ANY] * 8 + [VMEM] + [ANY] * 10,
+        scatter_buffers(
+            [(2 * rows, ff_half), (2 * rows, ff_half), (2 * rows, q_half), (2 * rows, qkv_half)], early_sums, zn
+        )
         + total_buffers(count, width) * 2
-        + [DMA((4,)), DMA((2,)), DMA((3,)), DMA((2,)), DMA((2, 2)), DMA((2, 4)), DMA((2, 2))]
-        + scatter_sems(2, 2, zn),
-        order=range(8),
-    )
-    branch = branch.reshape(chip, width)
-
-    q_sum, kv_sum, o_sum, up_sum, in_grad, gain_sums = call(
-        functools.partial(scatter_attention, zn, early_sums),
-        "scatter_attention",
-        3,
-        (
-            normed,
-            qkv_back,
-            branch,
-            context,
-            normed_two,
-            up_grad,
-            in_term,
-            mid_grad,
-            tokens,
-            gain_one,
-            gain_two_grad,
-        ),
-        [ANY] * 8 + [VMEM] * 3,
-        [
-            ((rows, 2 * q_half), F32),
-            ((2, rows, 2 * kv_half), F32),
-            ((rows, 2 * q_half), F32),
-            ((rows, 2 * ff_half), F32),
-            ((count, width), BF16),
-            ((8, 4 * rows), F32),
-            ((zn, 4 * rows, qkv_half), BF16),
-            ((zn, 4 * rows, q_half), BF16),
-            ((zn, 4 * rows, ff_half), BF16),
-        ],
-        [ANY] * 5 + [VMEM] + [ANY] * 3,
-        scatter_buffers([(2 * rows, ff_half), (2 * rows, q_half), (2 * rows, qkv_half)], early_sums, zn)
-        + total_buffers(count, width)
+        + [pltpu.VMEM((count, width), BF16)] * 2
+        + [DMA((5,))]
         + gain_buffers(zn, 4 * rows)
-        + [DMA((6,)), DMA((1,)), pltpu.VMEM((1, width), F32)]
-        + scatter_sems(3, 4, zn),
-        order=range(6),
+        + [pltpu.VMEM((1, width), F32)] * 2
+        + [
+            DMA((4,)),
+            DMA((2,)),
+            DMA((3,)),
+            DMA((2,)),
+            DMA((2, 2)),
+            DMA((2, 4)),
+            DMA((2, 2)),
+            pltpu.SemaphoreType.REGULAR,
+        ]
+        + scatter_sems(5, 6, zn),
+        order=range(9),
     )
     gain_grads = lax.dynamic_slice_in_dim(gain_sums, lax.rem(lax.axis_index("dp"), 4) * rows, rows, 1)
     return (

time: 557 us -> 529 us (0.950)
  Pallas kernels: 528 us -> 500 us
    pallas_call x3 -> x2, Pallas kernels: 528 us -> 500 us  [call(): pl.pallas_call(kernel, out_shape=[jax.ShapeDtypeStruct(shape, dtype) for...]
    unnamed x23 -> x21, local copies, waits for them, and re-layouts: 16.2 us -> 17.3 us
where the time goes in v2:
time: 529 us; the launch traced here: 528 us
  Pallas kernels  500 us (95%)
  local copies, waits for them, and re-layouts  23.2 us (4%)
    pallas_call x2, Pallas kernels, call(): pl.pallas_call(kernel, out_shape=[jax.ShapeDtypeStruct(shape, dtype) for...  500 us
    unnamed x21, local copies, waits for them, and re-layouts  17.3 us

profile of v2, /device:TPU:0, one launch (start us, length us, event | category | flops | bytes accessed | tf_op | source)
XLA Modules:
  0.0 527.7 jit_solution(11750976499591367052)
XLA Ops:
  0.6 2.2 copy.33
  2.9 1.8 copy.32
  4.7 0.9 copy.28
  5.5 0.1 copy.29
  5.7 0.9 copy.30
  6.5 0.1 copy.31
  6.7 0.7 pad_maximum_fusion.refs_1_
  7.4 0.7 bitcast_convert_fusion
  8.1 0.7 bitcast_convert_fusion.1
  8.8 0.6 pad_maximum_fusion.3.refs_3_
  9.4 0.6 reshape_tile.6.refs_10_
  10.0 0.7 broadcast_in_dim.4
  10.7 0.1 tile.14
  10.8 0.6 reshape_tile.7.refs_11_
  11.4 261.6 %forward.1 = (bf16[2048,640]{1,0:T(8,128)(2,1)}, bf16[2048,512]{1,0:T(8,128)(2,1)}, f32[128,128]{1,0:T(8,128)}, bf16[2,512,2048]{2,1,0:T(8,128)(2,1)}, bf16[2,51...) custom-call(bf16[128,1024]{1,0:T(8,128)(2,1)} %refs_0_.1, ...), custom_call_target="tpu_custom_call" | custom-call | tf_op jit(solution)/shard_map/forward/pallas_call | solution.py:1565
  273.0 1.3 reshape.105.refs_16_
  274.3 238.8 %backward.1 = (f32[128,2816]{1,0:T(8,128)}, f32[128,2816]{1,0:T(8,128)}, f32[128,2816]{1,0:T(8,128)}, f32[128,1024]{1,0:T(8,128)}, f32[128,1024]{1,0:T(8,128)}, ...) custom-call(bf16[1024,2048]{1,0:T(8,128)(2,1)} %bitcast.30, ...), custom_call_target="tpu_custom_call" | custom-call | tf_op jit(solution)/shard_map/backward/pallas_call | solution.py:1565
  513.1 0.0 copy-start.4
  513.1 1.1 slice_bitcast_fusion.1
  514.2 0.8 pad_maximum_fusion.1
  514.9 2.9 copy.35
  517.8 0.0 copy-start
  517.8 0.0 copy-done.4
  517.9 1.0 copy.34
  518.8 0.7 constant_dynamic-slice_fusion
  519.5 0.5 slice_bitcast_fusion.4
  520.0 3.2 copy.42
  523.2 0.0 copy-done
  523.2 0.0 copy-start.3
  523.2 0.0 copy-start.2
  523.2 1.3 copy.43
  524.5 0.1 copy-done.3
  524.6 0.0 copy-start.1
  524.6 0.8 copy.44
  525.4 0.1 copy-done.2
  525.5 1.1 copy.45
  526.6 0.0 copy-done.1
  526.6 1.1 copy.46
  (4 shorter events, 0.0 us)
Async XLA Ops:
  513.1 4.8 copy-start.4
  517.8 5.4 %copy-start = (bf16[512,2048]{1,0:T(8,128)(2,1)S(1)}, bf16[512,2048]{1,0:T(8,128)(2,1)}, u32[]{:S(2)}) copy-start(bf16[512,2048]{1,0:T(8,128)(2,1)} %get-tuple-element.129) | copy-start | bytes 6291460
  523.2 1.4 copy-start.3
  523.2 2.3 copy-start.2
  524.6 2.0 copy-start.1

commit v3 on v2

--- a/solution.py
+++ b/solution.py
@@ -2,6 +2,7 @@
 
 import jax
 import jax.numpy as jnp
+import numpy as np
 from jax import lax
 from jax.experimental import pallas as pl
 from jax.experimental.pallas import tpu as pltpu
@@ -171,10 +172,11 @@
         ref = self.rows(j, o * 2 + 1 - x, True)
         return remote(ref, ref, self.bs.at[j, down, o], self.br.at[j, o], (d + 4 - 8 * down, t))
 
-    def start(self):
-        for s in range(len(self.sources)):
-            self.give(s).start()
-            self.keep(s).start()
+    def start(self, arrays):
+        for s, source in enumerate(self.sources):
+            if source[0] in arrays:
+                self.give(s).start()
+                self.keep(s).start()
 
     def ready(self, arrays):
         for j in arrays:
@@ -829,17 +831,43 @@
     ).astype(BF16)
 
 
+def transposed(src, dst):
+    def body(n):
+        at = pl.ds(pl.multiple_of(n * 128, 128), 128)
+        dst[:, at] = src[at, :].astype(F32).T.astype(BF16)
+
+    loop(src.shape[0] // 128, body)
+
+
 def forward(zn, early, *refs):
-    q, kv, o_shard, gains, tokens, grads, seg, gate, up, down, inverse, sign = refs[:12]
+    q, k_shard, v_shard, o_turned, gain_shards, tokens_in, grads_in, seg, gate_in, up_in, down_in, inverse, sign = refs[:13]
+    refs = refs[1:]
     qkv_all, o_all, gains_all, chip_tokens, chip_grads, seg_all = refs[12:18]
     gate_all, up_all, down_all, mid_out, normed_out, act_out, gate_grad_out, up_grad_out, back_out = refs[18:27]
     term, normed_one_out, turned_out, context_out, cosines_out, sines_out, gain_out = refs[27:34]
     total_refs = refs[34:38]
     normed, out_sems, pair_sems, load_sems, grad_sems, stage_sems, block_sems = refs[38:45]
     cosines, sines, seg_pair, gain_tiles, gain_rows, swap_sems, seg_sems = refs[45:52]
+    kv, gains, o_shard, down, tokens, grads, gate, up, down_turned, first_sems = refs[52:62]
     here = place()
-    c = here[4]
+    z, c = here[2], here[4]
+    firsts = [
+        pltpu.make_async_copy(src, dst, first_sems.at[n])
+        for n, (src, dst) in enumerate(
+            ((down_in, down_turned), (tokens_in, tokens), (gate_in, gate), (up_in, up), (grads_in, grads))
+        )
+    ]
+    for copy in firsts:
+        copy.start()
     enter(zn, here)
+    keys, values = k_shard[...].astype(F32), v_shard[...].astype(F32)
+    is_key = lanes(keys.shape) < HEAD_DIM
+    kv[0] = jnp.where(is_key, keys, pltpu.roll(values, HEAD_DIM, 1)).astype(BF16)
+    kv[1] = jnp.where(is_key, pltpu.roll(keys, HEAD_DIM, 1), values).astype(BF16)
+    for i in range(2):
+        gains[i] = jnp.zeros(gains.shape[1:], F32)
+        gains[i, pl.ds(0, 2), pl.ds(0, gain_shards.shape[1])] = gain_shards[...].astype(F32)
+    transposed(o_turned, o_shard)
     total = Total(here, term, *total_refs)
     q_half = q.shape[1] // 2
     work = Gather(
@@ -854,7 +882,7 @@
             ([(shard, False, 0, shard.shape[1] // 2)], full, early)
             for shard, full in ((down, down_all), (gate, gate_all), (up, up_all))
         ],
-        refs[52:],
+        refs[62:],
     )
     count, width = tokens.shape
     columns = gate_all.shape[1]
@@ -865,18 +893,26 @@
     swap = remote(seg, seg_pair.at[c], seg_sems.at[0], seg_sems.at[1], (here[0] + 1 - 2 * c, here[1]))
     swap.start()
     seg_pair[c] = seg[...]
-    work.start()
+    work.start(attention_set)
+    firsts[0].wait()
+    transposed(down_turned, down)
+    work.start([3])
     work.ready(attention_set)
     work.start_own(attention_set)
+    for copy in firsts[1:]:
+        copy.wait()
     shared = [
         share(here, src, dst, swap_sems.at[n])
         for n, (src, dst) in enumerate(((tokens, chip_tokens), (grads, chip_grads)))
     ]
-    for copies in shared:
-        for copy in copies:
-            copy.start()
-    work.ready([5])
-    work.start_own([5])
+    for copy in shared[0]:
+        copy.start()
+    work.start([4, 5])
+    for copy in shared[1]:
+        copy.start()
+    work.start_early([1, 2])
+    work.ready([3])
+    work.start_own([3])
     swap.wait()
     for i in range(blocks):
         row = seg_pair[i // per, pl.ds(i % per, 1)]
@@ -891,16 +927,13 @@
     ]
     for copy in saves:
         copy.start()
-    work.start_early([1, 2])
     work.relay(1, attention_set)
-    work.start_early([5])
-    work.ready([3])
-    work.start_own([3])
     work.relay(2, attention_set)
+    work.start_early([3])
     work.relays(3, attention_set)
-    work.start_early([3])
-    work.ready([4])
-    work.start_own([4])
+    work.ready([4, 5])
+    work.start_own([4, 5])
+    work.start_early([4])
     work.arrived(0)
     load = pltpu.make_async_copy(gains_all, gain_tiles, load_sems.at[0])
     load.start()
@@ -1017,10 +1050,6 @@
         for i in range(per):
             store_term(i, i % 2).wait()
         total.core().start()
-        work.relay(1, [3])
-        work.relay(2, [3])
-        work.relay(1, [5])
-        work.relay(2, [5])
         loop(per, own)
         for i in range(blocks - 2, blocks):
             for copy in stores(i, i % 2):
@@ -1037,10 +1066,10 @@
         pltpu.VMEM((2, block, width), BF16),
     )
     total.meet(False)
-    work.start_early([4])
+    for j in (3, 4):
+        work.relay(1, [j])
+        work.relay(2, [j])
     work.relays(3, [3])
-    work.relay(1, [4])
-    work.relay(2, [4])
 
     def sums(mid):
         total.pair().wait_recv()
@@ -1058,7 +1087,7 @@
             copy.start()
         save.wait()
 
-    def hidden(first, second, silu, slope, up_grad, inputs, result, stages, back_stage):
+    def hidden(first, second, silu, slope, upward, up_grad, inputs, result, stages, back_stage):
         def fetch_grads(i, slot):
             return pltpu.make_async_copy(
                 chip_grads.at[i // per, pl.ds(pl.multiple_of(lax.rem(i, per) * block, block), block)],
@@ -1070,6 +1099,9 @@
             return pl.ds(pl.multiple_of(i * block, block), block)
 
         fetch_grads(0, 0).start()
+        pl.run_scoped(sums, pltpu.VMEM((count, width), F32))
+        work.relays(3, [4])
+        work.start_early([5])
         work.arrived(3)
         load = pltpu.make_async_copy(down_all, first, load_sems.at[0])
         load.start()
@@ -1086,9 +1118,9 @@
             slope[at_block(i)] = product(inputs[slot], first[...])
 
         loop(blocks, hidden_block)
-        work.relays(3, [4])
-        pl.run_scoped(sums, pltpu.VMEM((count, width), F32))
-        work.relays(3, [5])
+        work.relay(1, [5])
+        work.relay(2, [5])
+        upward[...] = jnp.zeros_like(upward)
         work.arrived(4)
         load = pltpu.make_async_copy(gate_all, second, load_sems.at[1])
         load.start()
@@ -1114,10 +1146,24 @@
         loop(blocks, gate_block)
         save_up = pltpu.make_async_copy(up_grad, up_grad_out, out_sems.at[2])
         save_up.start()
-        work.arrived(5)
-        load = pltpu.make_async_copy(up_all, first, load_sems.at[0])
-        load.start()
-        load.wait()
+        work.relays(3, [5])
+        group = width // zn
+
+        def up_rows(k):
+            o = farthest_first(zn, z, zn - 1 - k)
+            at = pl.ds(pl.multiple_of(o * group, group), group)
+            work.x_late(5, o).wait_recv()
+            load = pltpu.make_async_copy(up_all.at[at], first.at[at], load_sems.at[0])
+            load.start()
+            load.wait()
+
+            def up_part(i):
+                rows = normed[i // per, at_block(lax.rem(i, per)), at]
+                upward[at_block(i)] += product(rows, first[at])
+
+            loop(blocks, up_part)
+
+        loop(zn, up_rows)
 
         def stores(i, slot):
             to = at_block(i)
@@ -1137,13 +1183,10 @@
                 for copy in stores(i - 2, slot):
                     copy.wait()
 
-            result[...] = product(normed[i // per, at_block(lax.rem(i, per))], first[...])
-
             def body(at):
                 to = pl.ds(pl.multiple_of(i * block + at.start, 16), at.size)
-                upward = result[at]
-                stages[slot, 0, at] = (silu[to] * upward).astype(BF16)
-                stages[slot, 1, at] = (slope[to] * upward).astype(BF16)
+                stages[slot, 0, at] = (silu[to] * upward[to]).astype(BF16)
+                stages[slot, 1, at] = (slope[to] * upward[to]).astype(BF16)
 
             by_rows(block, body)
             value = times_transposed(stages[slot, 1], second[...]) + times_transposed(
@@ -1164,6 +1207,7 @@
         hidden,
         pltpu.VMEM((width, columns), BF16),
         pltpu.VMEM((width, columns), BF16),
+        pltpu.VMEM((2 * count, columns), F32),
         pltpu.VMEM((2 * count, columns), F32),
         pltpu.VMEM((2 * count, columns), F32),
         pltpu.VMEM((2 * count, columns), BF16),
@@ -1636,15 +1680,10 @@
     early = 2 * rows // 48 * 8
     early_sums = max(16, 2 * rows // 128 * 16)
 
-    kv_shard = jnp.concatenate([halves(k_weight), halves(v_weight)], axis=2)
-    gain_rows = jnp.zeros((8, 128), F32)
-    gain_rows = gain_rows.at[0, :rows].set(attn_gain.astype(F32)).at[1, :rows].set(mlp_gain.astype(F32))
-    gain_shard = jnp.stack([gain_rows, gain_rows])
-
     chip = 2 * count
-    inverse = 1.0 / 10000.0 ** (jnp.arange(0, HEAD_DIM, 2, dtype=F32) / HEAD_DIM)
-    inverse = jnp.tile(inverse, 4).reshape(1, 2 * HEAD_DIM)
-    sign = jnp.tile(jnp.repeat(jnp.array([-1.0, 1.0], F32), HEAD_DIM // 2), 2).reshape(1, 2 * HEAD_DIM)
+    inverse = 1.0 / 10000.0 ** (np.arange(0, HEAD_DIM, 2, dtype=np.float32) / HEAD_DIM)
+    inverse = np.tile(inverse.astype(np.float32), 4)[None]
+    sign = np.tile(np.repeat(np.array([-1.0, 1.0], np.float32), HEAD_DIM // 2), 2)[None]
     (
         qkv_full,
         o_full,
@@ -1669,19 +1708,20 @@
         0,
         (
             q_weight,
-            kv_shard,
-            o_weight.T,
-            gain_shard,
+            k_weight,
+            v_weight,
+            o_weight,
+            jnp.stack([attn_gain, mlp_gain]),
             tokens,
             out_grad,
             seg_ids,
             gate_weight,
             up_weight,
-            down_weight.T,
+            down_weight,
             inverse,
             sign,
         ),
-        [VMEM] * 12,
+        [VMEM] * 5 + [ANY] * 2 + [VMEM] + [ANY] * 3 + [VMEM] * 2,
         [
             ((width, qkv_half), BF16),
             ((width, q_half), BF16),
@@ -1713,6 +1753,16 @@
             pltpu.VMEM((units * 16, 128), F32),
             pltpu.VMEM((8, width), F32),
             DMA((2, 3)),
+            DMA((5,)),
+            pltpu.VMEM((2, rows, 2 * kv_half), BF16),
+            pltpu.VMEM((2, 8, 128), F32),
+            pltpu.VMEM((rows, 2 * q_half), BF16),
+            pltpu.VMEM((rows, 2 * ff_half), BF16),
+            pltpu.VMEM((count, width), BF16),
+            pltpu.VMEM((count, width), BF16),
+            pltpu.VMEM((rows, 2 * ff_half), BF16),
+            pltpu.VMEM((rows, 2 * ff_half), BF16),
+            pltpu.VMEM((2 * ff_half, rows), BF16),
             DMA((5,)),
         ]
         + gather_sems(6, 7, zn),

time: 529 us -> 508 us (0.960)
  Pallas kernels: 500 us -> 489 us
  local copies, waits for them, and re-layouts: 23.2 us -> 15.1 us
    pallas_call x2, Pallas kernels: 500 us -> 489 us  [call(): pl.pallas_call(kernel, out_shape=[jax.ShapeDtypeStruct(shape, dtype) for...]
    unnamed x21 -> x17, local copies, waits for them, and re-layouts: 17.3 us -> 11.5 us
where the time goes in v3:
time: 508 us; the launch traced here: 506 us
  Pallas kernels  489 us (96%)
  local copies, waits for them, and re-layouts  15.1 us (3%)
    pallas_call x2, Pallas kernels, call(): pl.pallas_call(kernel, out_shape=[jax.ShapeDtypeStruct(shape, dtype) for...  489 us
    unnamed x17, local copies, waits for them, and re-layouts  11.5 us

profile of v3, /device:TPU:0, one launch (start us, length us, event | category | flops | bytes accessed | tf_op | source)
XLA Modules:
  0.0 506.5 jit_solution(10791683618427065371)
XLA Ops:
  0.6 1.2 pad_maximum_fusion.2.refs_4_
  1.8 251.0 %forward.1 = (bf16[2048,640]{1,0:T(8,128)(2,1)}, bf16[2048,512]{1,0:T(8,128)(2,1)}, f32[128,128]{1,0:T(8,128)}, bf16[2,512,2048]{2,1,0:T(8,128)(2,1)}, bf16[2,51...) custom-call(bf16[128,1024]{1,0:T(8,128)(2,1)} %refs_0_.1, ...), custom_call_target="tpu_custom_call" | custom-call | tf_op jit(solution)/shard_map/forward/pallas_call | solution.py:1609
  252.8 1.3 reshape.33.refs_16_
  254.1 237.7 %backward.1 = (f32[128,2816]{1,0:T(8,128)}, f32[128,2816]{1,0:T(8,128)}, f32[128,2816]{1,0:T(8,128)}, f32[128,1024]{1,0:T(8,128)}, f32[128,1024]{1,0:T(8,128)}, ...) custom-call(bf16[1024,2048]{1,0:T(8,128)(2,1)} %bitcast.19, ...), custom_call_target="tpu_custom_call" | custom-call | tf_op jit(solution)/shard_map/backward/pallas_call | solution.py:1609
  491.8 0.0 copy-start.4
  491.9 1.1 slice_bitcast_fusion.1
  492.9 0.8 pad_maximum_fusion
  493.7 2.9 copy.26
  496.6 0.0 copy-start
  496.6 0.0 copy-done.4
  496.6 1.0 copy.25
  497.6 0.7 constant_dynamic-slice_fusion
  498.3 0.5 slice_bitcast_fusion.4
  498.8 3.2 copy.32
  502.0 0.0 copy-done
  502.0 0.0 copy-start.3
  502.0 0.0 copy-start.2
  502.0 1.3 copy.33
  503.3 0.1 copy-done.3
  503.3 0.0 copy-start.1
  503.3 0.8 copy.34
  504.1 0.1 copy-done.2
  504.2 1.1 copy.35
  505.3 0.0 copy-done.1
  505.4 1.1 copy.36
Async XLA Ops:
  491.8 4.8 copy-start.4
  496.6 5.4 %copy-start = (bf16[512,2048]{1,0:T(8,128)(2,1)S(1)}, bf16[512,2048]{1,0:T(8,128)(2,1)}, u32[]{:S(2)}) copy-start(bf16[512,2048]{1,0:T(8,128)(2,1)} %get-tuple-element.94) | copy-start | bytes 6291460
  502.0 1.4 copy-start.3
  502.0 2.3 copy-start.2
  503.3 2.0 copy-start.1

commit v4 on v3

--- a/solution.py
+++ b/solution.py
@@ -843,12 +843,12 @@
     q, k_shard, v_shard, o_turned, gain_shards, tokens_in, grads_in, seg, gate_in, up_in, down_in, inverse, sign = refs[:13]
     refs = refs[1:]
     qkv_all, o_all, gains_all, chip_tokens, chip_grads, seg_all = refs[12:18]
-    gate_all, up_all, down_all, mid_out, normed_out, act_out, gate_grad_out, up_grad_out, back_out = refs[18:27]
-    term, normed_one_out, turned_out, context_out, cosines_out, sines_out, gain_out = refs[27:34]
-    total_refs = refs[34:38]
-    normed, out_sems, pair_sems, load_sems, grad_sems, stage_sems, block_sems = refs[38:45]
-    cosines, sines, seg_pair, gain_tiles, gain_rows, swap_sems, seg_sems = refs[45:52]
-    kv, gains, o_shard, down, tokens, grads, gate, up, down_turned, first_sems = refs[52:62]
+    gate_all, up_all, down_all, mid_out, normed_out, act_out, gate_grad_out, up_grad_out = refs[18:26]
+    term, normed_one_out, turned_out, context_out, cosines_out, sines_out, gain_out = refs[26:33]
+    total_refs = refs[33:37]
+    normed, out_sems, pair_sems, load_sems, grad_sems, stage_sems, block_sems = refs[37:44]
+    cosines, sines, seg_pair, gain_tiles, gain_rows, swap_sems, seg_sems = refs[44:51]
+    kv, gains, o_shard, down, tokens, grads, gate, up, down_turned, first_sems = refs[51:61]
     here = place()
     z, c = here[2], here[4]
     firsts = [
@@ -882,7 +882,7 @@
             ([(shard, False, 0, shard.shape[1] // 2)], full, early)
             for shard, full in ((down, down_all), (gate, gate_all), (up, up_all))
         ],
-        refs[62:],
+        refs[61:],
     )
     count, width = tokens.shape
     columns = gate_all.shape[1]
@@ -1087,7 +1087,7 @@
             copy.start()
         save.wait()
 
-    def hidden(first, second, silu, slope, upward, up_grad, inputs, result, stages, back_stage):
+    def hidden(first, second, silu, slope, upward, up_grad, inputs, result, stages):
         def fetch_grads(i, slot):
             return pltpu.make_async_copy(
                 chip_grads.at[i // per, pl.ds(pl.multiple_of(lax.rem(i, per) * block, block), block)],
@@ -1170,9 +1170,6 @@
             return (
                 pltpu.make_async_copy(stages.at[slot, 0], act_out.at[to], stage_sems.at[slot, 0]),
                 pltpu.make_async_copy(stages.at[slot, 1], gate_grad_out.at[to], stage_sems.at[slot, 1]),
-                pltpu.make_async_copy(
-                    back_stage.at[slot], back_out.at[i // per, at_block(lax.rem(i, per))], stage_sems.at[slot, 2]
-                ),
             )
 
         def up_block(i):
@@ -1189,10 +1186,6 @@
                 stages[slot, 1, at] = (slope[to] * upward[to]).astype(BF16)
 
             by_rows(block, body)
-            value = times_transposed(stages[slot, 1], second[...]) + times_transposed(
-                up_grad[at_block(i)], first[...]
-            )
-            back_stage[slot] = value.astype(BF16)
             for copy in stores(i, slot):
                 copy.start()
 
@@ -1214,7 +1207,6 @@
         pltpu.VMEM((2, block, width), BF16),
         pltpu.VMEM((block, columns), F32),
         pltpu.VMEM((2, 2, block, columns), BF16),
-        pltpu.VMEM((2, block, width), BF16),
     )
     work.finish()
     total.finish()
@@ -1230,12 +1222,13 @@
 
 
 def backward(zn, early, *refs):
-    normed_two, gate_grad, chip_grads, activated, back_term, down_all, mid_in, up_grad, normed_one, context = refs[:10]
-    turned_all, o_all, qkv_all, cosines, sines, tokens_in, rows_of, gain_rows = refs[10:18]
-    down_out, gate_out, up_out, o_out, q_out, kv_out, out, in_grad, gain_out = refs[18:27]
-    mid_grad_all, branch_all, qkv_back, in_term, out_term, down, gate, up, o_sums, qkv_sums = refs[27:37]
+    normed_two, gate_grad, chip_grads, activated, gate_all, up_all, down_all, mid_in, up_grad = refs[:9]
+    normed_one, context, turned_all, o_all, qkv_all, cosines, sines, tokens_in, rows_of, gain_rows = refs[9:19]
+    down_out, gate_out, up_out, o_out, q_out, kv_out, out, in_grad, gain_out = refs[19:28]
+    mid_grad_all, branch_all, qkv_back, in_term, out_term, back_term = refs[28:34]
+    down, gate, up, o_sums, qkv_sums = refs[34:39]
     n = SCATTER_BUFFERS
-    buffers, refs = refs[37 : 37 + 4 * n], refs[37 + 4 * n :]
+    buffers, refs = refs[39 : 39 + 4 * n], refs[39 + 4 * n :]
     back_refs, front_refs, in_refs = refs[:4], refs[4:8], refs[8:11]
     gain_refs, (one_sum, two_sum), refs = refs[11:15], refs[15:17], refs[17:]
     fetch_sems, out_sems, pair_sems, weight_sems, stage_sems, block_sems, back_sems, credit = refs[:8]
@@ -1270,77 +1263,92 @@
         ],
         refs[8:],
     )
-    back.start()
-
-    def out_terms(right_one, weights, stages):
-        block = weights.shape[1]
-
-        def fetch_weights(i, slot):
-            return pltpu.make_async_copy(
-                down_all.at[pl.ds(pl.multiple_of(i * block, block), block)], weights.at[slot], weight_sems.at[slot]
-            )
-
-        def stores(i, slot):
-            to = pl.ds(pl.multiple_of(i * block, block), block)
-            return [
-                pltpu.make_async_copy(
-                    stages.at[slot, pl.ds(half * (chip // 2), chip // 2)],
-                    out_term.at[half, :, to],
-                    stage_sems.at[slot, half],
-                )
-                for half in range(2)
-            ]
-
-        fetch_weights(0, 0).start()
-
-        def step(i):
-            slot = lax.rem(i, 2)
-            fetch_weights(i, slot).wait()
-
-            @pl.when(i + 1 < width // block)
-            def _():
-                fetch_weights(i + 1, 1 - slot).start()
-
-            @pl.when(i > 1)
-            def _():
-                for copy in stores(i - 2, slot):
+    def feature_terms(factors, term):
+        def run(*refs):
+            lefts, weights, stages = refs[:-2], refs[-2], refs[-1]
+            group = weights.shape[2]
+            loads = fetch([(left, ref) for (left, _), ref in zip(factors, lefts)], fetch_sems)
+
+            def fetch_weights(i, slot):
+                at = pl.ds(pl.multiple_of(i * group, group), group)
+                return [
+                    pltpu.make_async_copy(full.at[at], weights.at[slot, k], weight_sems.at[slot, k])
+                    for k, (_, full) in enumerate(factors)
+                ]
+
+            def stores(i, slot):
+                to = pl.ds(pl.multiple_of(i * group, group), group)
+                return [
+                    pltpu.make_async_copy(
+                        stages.at[slot, pl.ds(half * count, count)], term.at[half, :, to], stage_sems.at[slot, half]
+                    )
+                    for half in range(2)
+                ]
+
+            for copy in fetch_weights(0, 0):
+                copy.start()
+            for load in loads:
+                load.wait()
+
+            def step(i):
+                slot = lax.rem(i, 2)
+                for copy in fetch_weights(i, slot):
                     copy.wait()
 
-            stages[slot] = times_transposed(right_one[...], weights[slot]).astype(BF16)
-            for copy in stores(i, slot):
-                copy.start()
-
-        loop(width // block, step)
-        for i in range(width // block - 2, width // block):
-            for copy in stores(i, i % 2):
-                copy.wait()
-
-    def first_terms(left, right, stage, weights, stages):
-        for load in fetch(((chip_grads, left), (activated, right)), fetch_sems):
-            load.wait()
-        work.make(0, left, right, stage, back.meet)
-        load = fetch(((normed_two, left),), fetch_sems)[0]
-        for g in range(3):
-            work.early_third(0, g)
-        work.late_third(0, 0)
-        out_terms(right, weights, stages)
-        front.start()
-        load_right = pltpu.make_async_copy(gate_grad, right, fetch_sems.at[1])
-        load_right.start()
-        work.early_home(0)
-        work.late_third(0, 1)
-        work.late_third(0, 2)
-        load.wait()
-        load_right.wait()
-        work.make(1, left, right, stage)
+                @pl.when(i + 1 < width // group)
+                def _():
+                    for copy in fetch_weights(i + 1, 1 - slot):
+                        copy.start()
+
+                @pl.when(i > 1)
+                def _():
+                    for copy in stores(i - 2, slot):
+                        copy.wait()
+
+                value = times_transposed(lefts[0][...], weights[slot, 0])
+                for k in range(1, len(lefts)):
+                    value = value + times_transposed(lefts[k][...], weights[slot, k])
+                stages[slot] = value.astype(BF16)
+                for copy in stores(i, slot):
+                    copy.start()
+
+            loop(width // group, step)
+            for i in range(width // group - 2, width // group):
+                for copy in stores(i, i % 2):
+                    copy.wait()
+
+        pl.run_scoped(
+            run,
+            *[pltpu.VMEM((chip, wide), BF16)] * len(factors),
+            pltpu.VMEM((2, len(factors), 256, wide), BF16),
+            pltpu.VMEM((2, chip, 256), BF16),
+        )
 
     wide = down.shape[2]
     operands = [pltpu.VMEM((chip, width), BF16), pltpu.VMEM((chip, wide), BF16), pltpu.VMEM((2,) + down.shape[1:], BF16)]
-    pl.run_scoped(
-        first_terms, *operands, pltpu.VMEM((2, 256, wide), BF16), pltpu.VMEM((2, chip, 256), BF16)
-    )
+
+    def terms_of(j, left_all, right_all):
+        def run(left, right, stage):
+            for load in fetch(((left_all, left), (right_all, right)), fetch_sems):
+                load.wait()
+            work.make(j, left, right, stage)
+
+        pl.run_scoped(run, *operands)
+
+    terms_of(0, chip_grads, activated)
+    for g in range(3):
+        work.early_third(0, g)
+    feature_terms([(gate_grad, gate_all), (up_grad, up_all)], back_term)
+    back.start()
+    work.late_third(0, 0)
+    feature_terms([(activated, down_all)], out_term)
+    back.meet()
+    front.start()
+    work.late_third(0, 1)
+    work.early_home(0)
+    work.late_third(0, 2)
+    terms_of(1, normed_two, gate_grad)
     work.early_third(1, 0)
-    work.early_third(1, 1)
 
     def sums(mid, mid_grad, grads):
         for load in fetch(
@@ -1360,6 +1368,13 @@
             two_sum[...] += jnp.sum(back.half[at].astype(F32) * (value * factor), axis=0, keepdims=True)
 
         by_rows(count, body_gain)
+        work.late_third(1, 0)
+        work.early_third(1, 1)
+        work.early_third(1, 2)
+        work.home(0)
+        work.done(0)
+        work.lend(credit)
+        front.meet()
         back.pair().wait_recv()
 
         def body(at):
@@ -1379,16 +1394,12 @@
         save.start()
         for copy in share(here, branch, branch_all, pair_sems):
             copy.start()
-        work.early_third(1, 2)
+        work.late_third(1, 1)
         save.wait()
 
     pl.run_scoped(
         sums, pltpu.VMEM((count, width), F32), pltpu.VMEM((count, width), F32), pltpu.VMEM((count, width), BF16)
     )
-    work.home(0)
-    work.late_third(1, 0)
-    work.done(0)
-    work.lend(credit)
 
     def middle_terms(left, right, stage):
         for copy in share(here, branch, branch_all, pair_sems):
@@ -1404,8 +1415,8 @@
             load.wait()
         work.make(3, left, right_o, stage)
         loads = fetch(((normed_two, left), (up_grad, right)), fetch_sems)
-        front.meet()
-        work.late_third(1, 1)
+        work.early_third(3, 0)
+        work.late_third(1, 2)
         for load in loads:
             load.wait()
         work.borrow(credit)
@@ -1413,7 +1424,6 @@
 
     pl.run_scoped(middle_terms, *operands)
     work.early_third(2, 0)
-    work.late_third(1, 2)
 
     def attention(o, qkv, inputs, turned, grads, backs, terms_out, cosine, sine, accumulators):
         def which(i):
@@ -1459,15 +1469,16 @@
                     for copy in stores(done, done % 2):
                         copy.wait()
                 total.core().start()
-                work.early_home(1)
-                work.early_third(3, 0)
-                work.late_third(3, 0)
+                work.early_third(2, 2)
+
+            @pl.when(i == 1)
+            def _():
+                work.early_third(3, 1)
                 work.early_third(2, 1)
 
             @pl.when(i == blocks - 1)
             def _():
-                work.early_third(2, 2)
-                work.early_third(3, 1)
+                work.late_third(2, 0)
 
             for copy in fetches(i, slot):
                 copy.wait()
@@ -1515,7 +1526,6 @@
 
     def meeting(tokens):
         load = fetch(((tokens_in, tokens),), fetch_sems)[0]
-        work.late_third(3, 1)
         total.meet(send=False)
         load.wait()
         one_sum[...] = jnp.zeros_like(one_sum)
@@ -1531,8 +1541,26 @@
     gains.start([one_sum, two_sum])
     gains.swapped(0)
     total.pair().start()
-    work.late_third(3, 2)
-    work.late_third(2, 0)
+    work.early_third(3, 2)
+    work.late_third(2, 1)
+
+    def output(mid):
+        load = fetch(((mid_in, mid),), fetch_sems)[0]
+        front.pair().wait_recv()
+        load.wait()
+
+        def body_out(at):
+            out_rows[at] = (mid[at] + front.rows(at)).astype(BF16)
+
+        by_rows(count, body_out)
+
+    pl.run_scoped(output, pltpu.VMEM((count, width), F32))
+    save_out = pltpu.make_async_copy(out_rows, out, out_sems.at[1])
+    save_out.start()
+    work.late_third(3, 0)
+    work.late_third(2, 2)
+    work.early_home(2)
+    work.early_home(1)
 
     def last_terms(left, right, stage):
         right_qkv = right.at[:, pl.ds(0, qkv_wide)]
@@ -1543,31 +1571,19 @@
 
     pl.run_scoped(last_terms, *operands)
     work.early_third(4, 0)
+    work.home(1)
+    work.late_third(4, 0)
     work.early_third(4, 1)
-    work.late_third(2, 1)
-    work.early_third(3, 2)
-    work.late_third(2, 2)
-
-    def output(mid):
-        load = fetch(((mid_in, mid),), fetch_sems)[0]
-        front.pair().wait_recv()
-        load.wait()
-
-        def body_out(at):
-            out_rows[at] = (mid[at] + front.rows(at)).astype(BF16)
-
-        by_rows(count, body_out)
-
-    pl.run_scoped(output, pltpu.VMEM((count, width), F32))
-    save_out = pltpu.make_async_copy(out_rows, out, out_sems.at[1])
-    save_out.start()
-    work.home(1)
-    work.early_home(2)
+    work.early_third(4, 2)
     work.early_home(3)
-    work.early_third(4, 2)
-    work.late_third(4, 0)
+    work.late_third(3, 1)
+    work.home(2)
     gains.swapped(2)
     gains.run()
+    work.late_third(4, 1)
+    work.late_third(4, 2)
+    work.late_third(3, 2)
+    work.early_home(4)
 
     def inputs_back(mid_grad, tokens):
         loads = fetch(((mid_grad_all, mid_grad), (tokens_in, tokens)), fetch_sems)
@@ -1591,18 +1607,61 @@
     pl.run_scoped(inputs_back, pltpu.VMEM((count, width), F32), pltpu.VMEM((count, width), BF16))
     save_in = pltpu.make_async_copy(in_rows, in_grad, out_sems.at[0])
     save_in.start()
-    work.late_third(4, 1)
-    work.late_third(4, 2)
-    work.early_home(4)
     gains.finish(gain_out)
-    for j in (2, 3, 4):
-        work.home(j)
+    work.home(4)
+    work.home(3)
     for j in (1, 2, 3, 4):
         work.done(j)
     front.finish()
     total.finish()
     save_out.wait()
     save_in.wait()
+
+
+def settle(*refs):
+    turned, plain, kv = refs[:2], refs[2:7], refs[7]
+    turned_out, plain_out, (k_out, v_out) = refs[8:10], refs[10:15], refs[15:17]
+    turned_in, turned_to, plain_at, (kv_at, k_at, v_at) = refs[17:19], refs[19:21], refs[21:26], refs[26:29]
+    load_sems, store_sems = refs[29:]
+
+    def load(n, src, dst):
+        return pltpu.make_async_copy(src, dst, load_sems.at[n])
+
+    def store(n, src, dst):
+        return pltpu.make_async_copy(src, dst, store_sems.at[n])
+
+    loads = [load(0, turned[0], turned_in[0]), load(1, turned[1], turned_in[1]), load(2, kv, kv_at)]
+    loads += [load(3 + n, src, dst) for n, (src, dst) in enumerate(zip(plain, plain_at))]
+    for copy in loads[3:] + loads[:3]:
+        copy.start()
+    stores = []
+
+    def send(n, src, dst):
+        stores.append(store(n, src, dst))
+        stores[-1].start()
+
+    for n in range(5):
+        loads[3 + n].wait()
+        send(4 + n, plain_at[n], plain_out[n])
+    for n in range(2):
+        loads[n].wait()
+        src, dst = turned_in[n], turned_to[n]
+
+        def body(i, src=src, dst=dst):
+            at = pl.ds(pl.multiple_of(i * 128, 128), 128)
+            dst[at, :] = src[:, at].T
+
+        loop(src.shape[1] // 128, body)
+        send(n, dst, turned_out[n])
+    loads[2].wait()
+    one, two = kv_at[0], kv_at[1]
+    is_key = lanes(one.shape) < HEAD_DIM
+    k_at[...] = jnp.where(is_key, one, pltpu.roll(two, HEAD_DIM, 1))
+    v_at[...] = jnp.where(is_key, pltpu.roll(one, HEAD_DIM, 1), two)
+    send(2, k_at, k_out)
+    send(3, v_at, v_out)
+    for copy in stores:
+        copy.wait()
 
 
 def call(kernel, name, collective_id, operands, specs, outs, out_specs, scratch, order=None):
@@ -1614,7 +1673,7 @@
         scratch_shapes=scratch,
         name=name,
         compiler_params=pltpu.CompilerParams(
-            collective_id=collective_id, has_side_effects=True, vmem_limit_bytes=63 << 20
+            collective_id=collective_id, has_side_effects=True, vmem_limit_bytes=255 << 18
         ),
     )(*operands)
     return results if order is None else [results[i] for i in order]
@@ -1678,7 +1737,7 @@
     qkv_half = q_half + 2 * kv_half
     heads, groups = q_half // HEAD_DIM, kv_half // HEAD_DIM
     early = 2 * rows // 48 * 8
-    early_sums = max(16, 2 * rows // 128 * 16)
+    early_sums = max(16, 2 * rows * 3 // 256 * 16)
 
     chip = 2 * count
     inverse = 1.0 / 10000.0 ** (np.arange(0, HEAD_DIM, 2, dtype=np.float32) / HEAD_DIM)
@@ -1689,13 +1748,14 @@
         o_full,
         grads_chip,
         segment,
+        gate_full,
+        up_full,
         down_full,
         mid,
         normed_two,
         activated,
         gate_grad,
         up_grad,
-        back_term,
         normed,
         turned,
         context,
@@ -1733,11 +1793,11 @@
         + [((width, ff_half), BF16)] * 3
         + [((count, width), F32), ((2, count, width), BF16)]
         + [((chip, ff_half), BF16)] * 3
-        + [((2, count, width), BF16)] * 2
+        + [((2, count, width), BF16)]
         + [((chip, width), BF16), ((chip, qkv_half), BF16), ((chip, q_half), BF16)]
         + [((chip, 2 * HEAD_DIM), F32)] * 2
         + [((8, width), F32)],
-        [ANY] * 22,
+        [ANY] * 21,
         total_buffers(count, width)
         + [
             pltpu.VMEM((2, count, width), BF16),
@@ -1766,7 +1826,7 @@
             DMA((5,)),
         ]
         + gather_sems(6, 7, zn),
-        order=(0, 1, 4, 5, 8, 9, 10, 11, 12, 13, 14, 16, 17, 18, 19, 20, 21),
+        order=(0, 1, 4, 5, 6, 7, 8, 9, 10, 11, 12, 13, 15, 16, 17, 18, 19, 20),
     )
     grads_chip = grads_chip.reshape(chip, width)
     segment = segment.reshape(blocks, 1, block_rows)
@@ -1781,7 +1841,8 @@
             gate_grad,
             grads_chip,
             activated,
-            back_term,
+            gate_full,
+            up_full,
             down_full,
             mid,
             up_grad,
@@ -1796,7 +1857,7 @@
             segment,
             gain_rows,
         ),
-        [ANY] * 16 + [VMEM] * 2,
+        [ANY] * 17 + [VMEM] * 2,
         [((rows, 2 * ff_half), F32)] * 3
         + [
             ((rows, 2 * q_half), F32),
@@ -1810,10 +1871,11 @@
             ((chip, qkv_half), BF16),
             ((2, count, width), BF16),
             ((2, count, width), BF16),
+            ((2, count, width), BF16),
         ]
         + [((zn, 4 * rows, ff_half), BF16)] * 3
         + [((zn, 4 * rows, q_half), BF16), ((zn, 4 * rows, qkv_half), BF16)],
-        [ANY] * 8 + [VMEM] + [ANY] * 10,
+        [ANY] * 8 + [VMEM] + [ANY] * 11,
         scatter_buffers(
             [(2 * rows, ff_half), (2 * rows, ff_half), (2 * rows, q_half), (2 * rows, qkv_half)], early_sums, zn
         )
@@ -1826,7 +1888,7 @@
             DMA((4,)),
             DMA((2,)),
             DMA((3,)),
-            DMA((2,)),
+            DMA((2, 2)),
             DMA((2, 2)),
             DMA((2, 4)),
             DMA((2, 2)),
@@ -1836,17 +1898,37 @@
         order=range(9),
     )
     gain_grads = lax.dynamic_slice_in_dim(gain_sums, lax.rem(lax.axis_index("dp"), 4) * rows, rows, 1)
+    plain = (gate_sum, up_sum, q_sum, out, in_grad)
+    turned = (down_sum, o_sum)
+    shapes = [ref.shape[::-1] for ref in turned]
+    results = pl.pallas_call(
+        settle,
+        out_shape=[jax.ShapeDtypeStruct(shape, F32) for shape in shapes]
+        + [jax.ShapeDtypeStruct(ref.shape, ref.dtype) for ref in plain]
+        + [jax.ShapeDtypeStruct((rows, 2 * kv_half), F32)] * 2,
+        in_specs=[pl.BlockSpec(memory_space=pltpu.HBM)] * 8,
+        out_specs=[pl.BlockSpec(memory_space=pltpu.HBM)] * 9,
+        scratch_shapes=[pltpu.VMEM(ref.shape, F32) for ref in turned]
+        + [pltpu.VMEM(shape, F32) for shape in shapes]
+        + [pltpu.VMEM(ref.shape, ref.dtype) for ref in plain]
+        + [pltpu.VMEM(kv_sum.shape, F32)]
+        + [pltpu.VMEM((rows, 2 * kv_half), F32)] * 2
+        + [DMA((8,)), DMA((9,))],
+        name="settle",
+        compiler_params=pltpu.CompilerParams(vmem_limit_bytes=62 << 20),
+    )(*turned, *plain, kv_sum)
+    down_final, o_final, gate_final, up_final, q_final, out, in_grad, k_final, v_final = results
     return (
         out,
         in_grad,
-        q_sum,
-        joined(kv_sum[:, :, :kv_half]),
-        joined(kv_sum[:, :, kv_half:]),
-        o_sum.T,
+        q_final,
+        k_final,
+        v_final,
+        o_final,
         gain_grads[0],
-        gate_sum,
-        up_sum,
-        down_sum.T,
+        gate_final,
+        up_final,
+        down_final,
         gain_grads[1],
     )
 

time: 508 us -> 494 us (0.972)
  local copies, waits for them, and re-layouts: 15.1 us -> 2.48 us
    unnamed x17 -> x0, local copies, waits for them, and re-layouts: 11.5 us -> none
    pallas_call x2, Pallas kernels: 489 us -> 479 us  [call(): pl.pallas_call(kernel, out_shape=[jax.ShapeDtypeStruct(shape, dtype) for...]
    pallas_call x0 -> x1, Pallas kernels: none -> 9.58 us  [local(): pl.pallas_call(settle, out_shape=[jax.ShapeDtypeStruct(shape, F32) for sh...]
where the time goes in v4:
time: 494 us; the launch traced here: 493 us
  Pallas kernels  488 us (99%)
    pallas_call x2, Pallas kernels, call(): pl.pallas_call(kernel, out_shape=[jax.ShapeDtypeStruct(shape, dtype) for...  479 us

profile of v4, /device:TPU:0, one launch (start us, length us, event | category | flops | bytes accessed | tf_op | source)
XLA Modules:
  0.0 492.8 jit_solution(3393138922985094640)
XLA Ops:
  0.6 1.2 pad_maximum_fusion.refs_4_
  1.8 237.6 %forward.1 = (bf16[2048,640]{1,0:T(8,128)(2,1)}, bf16[2048,512]{1,0:T(8,128)(2,1)}, f32[128,128]{1,0:T(8,128)}, bf16[2,512,2048]{2,1,0:T(8,128)(2,1)}, bf16[2,51...) custom-call(bf16[128,1024]{1,0:T(8,128)(2,1)} %refs_0_.1, ...), custom_call_target="tpu_custom_call" | custom-call | tf_op jit(solution)/shard_map/forward/pallas_call | solution.py:1668
  239.4 1.3 reshape.33.refs_17_
  240.7 241.3 %backward.1 = (f32[128,2816]{1,0:T(8,128)}, f32[128,2816]{1,0:T(8,128)}, f32[128,2816]{1,0:T(8,128)}, f32[128,1024]{1,0:T(8,128)}, f32[128,1024]{1,0:T(8,128)}, ...) custom-call(bf16[1024,2048]{1,0:T(8,128)(2,1)} %bitcast.9, ...), custom_call_target="tpu_custom_call" | custom-call | tf_op jit(solution)/shard_map/backward/pallas_call | solution.py:1668
  482.0 9.6 %settle.1 = (f32[2816,128]{1,0:T(8,128)}, f32[1024,128]{1,0:T(8,128)}, f32[128,2816]{1,0:T(8,128)}, f32[128,2816]{1,0:T(8,128)}, f32[128,1024]{1,0:T(8,128)}, /*...) custom-call(f32[128,2816]{1,0:T(8,128)} %get-tuple-element.65.refs_0_, ...), custom_call_target="tpu_custom_call" | custom-call | tf_op jit(solution)/shard_map/settle/pallas_call | solution.py:1904
  491.6 0.7 constant_dynamic-slice_fusion
  492.3 0.5 slice_bitcast_fusion

commit v5 on v4

--- a/solution.py
+++ b/solution.py
@@ -840,8 +840,8 @@
 
 
 def forward(zn, early, *refs):
-    q, k_shard, v_shard, o_turned, gain_shards, tokens_in, grads_in, seg, gate_in, up_in, down_in, inverse, sign = refs[:13]
-    refs = refs[1:]
+    q, k_shard, v_shard, o_turned, one_shard, two_shard, tokens_in, grads_in, seg, gate_in, up_in, down_in, inverse, sign = refs[:14]
+    refs = refs[2:]
     qkv_all, o_all, gains_all, chip_tokens, chip_grads, seg_all = refs[12:18]
     gate_all, up_all, down_all, mid_out, normed_out, act_out, gate_grad_out, up_grad_out = refs[18:26]
     term, normed_one_out, turned_out, context_out, cosines_out, sines_out, gain_out = refs[26:33]
@@ -866,7 +866,8 @@
     kv[1] = jnp.where(is_key, pltpu.roll(keys, HEAD_DIM, 1), values).astype(BF16)
     for i in range(2):
         gains[i] = jnp.zeros(gains.shape[1:], F32)
-        gains[i, pl.ds(0, 2), pl.ds(0, gain_shards.shape[1])] = gain_shards[...].astype(F32)
+        for k, shard in enumerate((one_shard, two_shard)):
+            gains[i, pl.ds(k, 1), pl.ds(0, shard.shape[1])] = shard[...].astype(F32)
     transposed(o_turned, o_shard)
     total = Total(here, term, *total_refs)
     q_half = q.shape[1] // 2
@@ -1495,7 +1496,7 @@
                 backs.at[slot],
                 accumulators,
                 q_half,
-                rows_of[which(i)],
+                rows_of[which(i) // per, pl.ds(lax.rem(which(i), per), 1)],
                 cosine[slot],
                 sine[slot],
             )
@@ -1619,47 +1620,62 @@
 
 
 def settle(*refs):
-    turned, plain, kv = refs[:2], refs[2:7], refs[7]
-    turned_out, plain_out, (k_out, v_out) = refs[8:10], refs[10:15], refs[15:17]
-    turned_in, turned_to, plain_at, (kv_at, k_at, v_at) = refs[17:19], refs[19:21], refs[21:26], refs[26:29]
-    load_sems, store_sems = refs[29:]
-
-    def load(n, src, dst):
-        return pltpu.make_async_copy(src, dst, load_sems.at[n])
-
-    def store(n, src, dst):
-        return pltpu.make_async_copy(src, dst, store_sems.at[n])
-
-    loads = [load(0, turned[0], turned_in[0]), load(1, turned[1], turned_in[1]), load(2, kv, kv_at)]
-    loads += [load(3 + n, src, dst) for n, (src, dst) in enumerate(zip(plain, plain_at))]
-    for copy in loads[3:] + loads[:3]:
-        copy.start()
+    turned, plain, kv, gains = refs[:2], refs[2:7], refs[7], refs[8]
+    turned_out, plain_out, (k_out, v_out, one_out, two_out) = refs[9:11], refs[11:16], refs[16:20]
+    turned_in, turned_to, plain_at, (kv_at, k_at, v_at) = refs[20:22], refs[22:24], refs[24:29], refs[29:32]
+    load_sems, store_sems = refs[32:]
+    pairs = list(zip(plain, plain_at)) + list(zip(turned, turned_in)) + [(kv, kv_at)]
+    loads = [pltpu.make_async_copy(src, dst, load_sems.at[n]) for n, (src, dst) in enumerate(pairs)]
+    for n in (0, 1, 5, 3, 4, 2, 6, 7):
+        loads[n].start()
     stores = []
 
-    def send(n, src, dst):
-        stores.append(store(n, src, dst))
+    def send(src, dst):
+        stores.append(pltpu.make_async_copy(src, dst, store_sems.at[len(stores)]))
         stores[-1].start()
 
-    for n in range(5):
-        loads[3 + n].wait()
-        send(4 + n, plain_at[n], plain_out[n])
-    for n in range(2):
+    def pass_on(n):
         loads[n].wait()
+        send(plain_at[n], plain_out[n])
+
+    def turn(n, first, last):
         src, dst = turned_in[n], turned_to[n]
 
-        def body(i, src=src, dst=dst):
-            at = pl.ds(pl.multiple_of(i * 128, 128), 128)
+        def body(i):
+            at = pl.ds(pl.multiple_of((first + i) * 128, 128), 128)
             dst[at, :] = src[:, at].T
 
-        loop(src.shape[1] // 128, body)
-        send(n, dst, turned_out[n])
-    loads[2].wait()
+        loop(last - first, body)
+
+    pass_on(0)
+    pass_on(1)
+    groups = turned_in[0].shape[1] // 128
+    loads[5].wait()
+    turn(0, 0, groups // 2)
+    pass_on(3)
+    pass_on(4)
+    turn(0, groups // 2, groups)
+    send(turned_to[0], turned_out[0])
+    pass_on(2)
+    loads[6].wait()
+    turn(1, 0, turned_in[1].shape[1] // 128)
+    send(turned_to[1], turned_out[1])
+    loads[7].wait()
     one, two = kv_at[0], kv_at[1]
     is_key = lanes(one.shape) < HEAD_DIM
     k_at[...] = jnp.where(is_key, one, pltpu.roll(two, HEAD_DIM, 1))
     v_at[...] = jnp.where(is_key, pltpu.roll(one, HEAD_DIM, 1), two)
-    send(2, k_at, k_out)
-    send(3, v_at, v_out)
+    send(k_at, k_out)
+    send(v_at, v_out)
+    features = one_out.shape[1]
+    for owner in range(4):
+
+        @pl.when(lax.rem(lax.axis_index("dp"), 4) == owner)
+        def _():
+            at = pl.ds(owner * features, features)
+            one_out[...] = gains[pl.ds(0, 1), at]
+            two_out[...] = gains[pl.ds(1, 1), at]
+
     for copy in stores:
         copy.wait()
 
@@ -1771,7 +1787,8 @@
             k_weight,
             v_weight,
             o_weight,
-            jnp.stack([attn_gain, mlp_gain]),
+            attn_gain[None],
+            mlp_gain[None],
             tokens,
             out_grad,
             seg_ids,
@@ -1781,7 +1798,7 @@
             inverse,
             sign,
         ),
-        [VMEM] * 5 + [ANY] * 2 + [VMEM] + [ANY] * 3 + [VMEM] * 2,
+        [VMEM] * 6 + [ANY] * 2 + [VMEM] + [ANY] * 3 + [VMEM] * 2,
         [
             ((width, qkv_half), BF16),
             ((width, q_half), BF16),
@@ -1829,7 +1846,6 @@
         order=(0, 1, 4, 5, 6, 7, 8, 9, 10, 11, 12, 13, 15, 16, 17, 18, 19, 20),
     )
     grads_chip = grads_chip.reshape(chip, width)
-    segment = segment.reshape(blocks, 1, block_rows)
     normed_two = normed_two.reshape(chip, width)
 
     down_sum, gate_sum, up_sum, o_sum, q_sum, kv_sum, out, in_grad, gain_sums = call(
@@ -1897,7 +1913,6 @@
         + scatter_sems(5, 6, zn),
         order=range(9),
     )
-    gain_grads = lax.dynamic_slice_in_dim(gain_sums, lax.rem(lax.axis_index("dp"), 4) * rows, rows, 1)
     plain = (gate_sum, up_sum, q_sum, out, in_grad)
     turned = (down_sum, o_sum)
     shapes = [ref.shape[::-1] for ref in turned]
@@ -1905,9 +1920,10 @@
         settle,
         out_shape=[jax.ShapeDtypeStruct(shape, F32) for shape in shapes]
         + [jax.ShapeDtypeStruct(ref.shape, ref.dtype) for ref in plain]
-        + [jax.ShapeDtypeStruct((rows, 2 * kv_half), F32)] * 2,
-        in_specs=[pl.BlockSpec(memory_space=pltpu.HBM)] * 8,
-        out_specs=[pl.BlockSpec(memory_space=pltpu.HBM)] * 9,
+        + [jax.ShapeDtypeStruct((rows, 2 * kv_half), F32)] * 2
+        + [jax.ShapeDtypeStruct((1, rows), F32)] * 2,
+        in_specs=[pl.BlockSpec(memory_space=pltpu.HBM)] * 8 + [VMEM],
+        out_specs=[pl.BlockSpec(memory_space=pltpu.HBM)] * 9 + [VMEM] * 2,
         scratch_shapes=[pltpu.VMEM(ref.shape, F32) for ref in turned]
         + [pltpu.VMEM(shape, F32) for shape in shapes]
         + [pltpu.VMEM(ref.shape, ref.dtype) for ref in plain]
@@ -1916,8 +1932,8 @@
         + [DMA((8,)), DMA((9,))],
         name="settle",
         compiler_params=pltpu.CompilerParams(vmem_limit_bytes=62 << 20),
-    )(*turned, *plain, kv_sum)
-    down_final, o_final, gate_final, up_final, q_final, out, in_grad, k_final, v_final = results
+    )(*turned, *plain, kv_sum, gain_sums)
+    down_final, o_final, gate_final, up_final, q_final, out, in_grad, k_final, v_final, one, two = results
     return (
         out,
         in_grad,
@@ -1925,11 +1941,11 @@
         k_final,
         v_final,
         o_final,
-        gain_grads[0],
+        one.reshape(rows),
         gate_final,
         up_final,
         down_final,
-        gain_grads[1],
+        two.reshape(rows),
     )
 
 

time: 494 us -> 489 us (0.990)
  no operation moved by 1% of the time
where the time goes in v5:
time: 489 us
  Pallas kernels  488 us (100%)
    pallas_call x2, Pallas kernels, call(): pl.pallas_call(kernel, out_shape=[jax.ShapeDtypeStruct(shape, dtype) for...  479 us

profile of v5, /device:TPU:0, one launch (start us, length us, event | category | flops | bytes accessed | tf_op | source)
XLA Modules:
  0.0 488.6 jit_solution(7910630622182216652)
XLA Ops:
  0.6 237.7 %forward.1 = (bf16[2048,640]{1,0:T(8,128)(2,1)}, bf16[2048,512]{1,0:T(8,128)(2,1)}, f32[128,128]{1,0:T(8,128)}, bf16[2,512,2048]{2,1,0:T(8,128)(2,1)}, bf16[2,51...) custom-call(bf16[128,1024]{1,0:T(8,128)(2,1)} %refs_0_.1, ...), custom_call_target="tpu_custom_call" | custom-call | tf_op jit(solution)/shard_map/forward/pallas_call | solution.py:1684
  238.3 241.4 %backward.1 = (f32[128,2816]{1,0:T(8,128)}, f32[128,2816]{1,0:T(8,128)}, f32[128,2816]{1,0:T(8,128)}, f32[128,1024]{1,0:T(8,128)}, f32[128,1024]{1,0:T(8,128)}, ...) custom-call(bf16[1024,2048]{1,0:T(8,128)(2,1)} %bitcast.7, ...), custom_call_target="tpu_custom_call" | custom-call | tf_op jit(solution)/shard_map/backward/pallas_call | solution.py:1684
  479.8 8.6 %settle.1 = (f32[2816,128]{1,0:T(8,128)}, f32[1024,128]{1,0:T(8,128)}, f32[128,2816]{1,0:T(8,128)}, f32[128,2816]{1,0:T(8,128)}, f32[128,1024]{1,0:T(8,128)}, /*...) custom-call(f32[128,2816]{1,0:T(8,128)} %get-tuple-element.67.refs_0, ...), custom_call_target="tpu_custom_call" | custom-call | tf_op jit(solution)/shard_map/settle/pallas_call | solution.py:1919

commit v6 on v5

--- a/solution.py
+++ b/solution.py
@@ -876,12 +876,12 @@
         here,
         [
             ([(gains, True, 0, gains.shape[2])], gains_all, 0),
-            ([(q, False, 0, q_half), (kv, True, q_half, kv.shape[2])], qkv_all, early),
-            ([(o_shard, False, 0, o_shard.shape[1] // 2)], o_all, early),
+            ([(q, False, 0, q_half), (kv, True, q_half, kv.shape[2])], qkv_all, early[0]),
+            ([(o_shard, False, 0, o_shard.shape[1] // 2)], o_all, early[0]),
         ]
         + [
-            ([(shard, False, 0, shard.shape[1] // 2)], full, early)
-            for shard, full in ((down, down_all), (gate, gate_all), (up, up_all))
+            ([(shard, False, 0, shard.shape[1] // 2)], full, rows_early)
+            for shard, full, rows_early in zip((down, gate, up), (down_all, gate_all, up_all), early[1:])
         ],
         refs[61:],
     )
@@ -1752,7 +1752,7 @@
     ff_half = gate_weight.shape[1] // 2
     qkv_half = q_half + 2 * kv_half
     heads, groups = q_half // HEAD_DIM, kv_half // HEAD_DIM
-    early = 2 * rows // 48 * 8
+    early = [2 * rows * part // 256 // 8 * 8 for part in (32, 40, 32, 48)]
     early_sums = max(16, 2 * rows * 3 // 256 * 16)
 
     chip = 2 * count

time: 489 us -> 488 us (level)
  no operation moved by 1% of the time
where the time goes in v6:
time: 488 us
  Pallas kernels  487 us (100%)
    pallas_call x2, Pallas kernels, call(): pl.pallas_call(kernel, out_shape=[jax.ShapeDtypeStruct(shape, dtype) for...  478 us

profile of v6, /device:TPU:0, one launch (start us, length us, event | category | flops | bytes accessed | tf_op | source)
XLA Modules:
  0.0 487.5 jit_solution(14614564337058002371)
XLA Ops:
  0.6 237.8 %forward.1 = (bf16[2048,640]{1,0:T(8,128)(2,1)}, bf16[2048,512]{1,0:T(8,128)(2,1)}, f32[128,128]{1,0:T(8,128)}, bf16[2,512,2048]{2,1,0:T(8,128)(2,1)}, bf16[2,51...) custom-call(bf16[128,1024]{1,0:T(8,128)(2,1)} %refs_0_.1, ...), custom_call_target="tpu_custom_call" | custom-call | tf_op jit(solution)/shard_map/forward/pallas_call | solution.py:1684
  238.4 240.2 %backward.1 = (f32[128,2816]{1,0:T(8,128)}, f32[128,2816]{1,0:T(8,128)}, f32[128,2816]{1,0:T(8,128)}, f32[128,1024]{1,0:T(8,128)}, f32[128,1024]{1,0:T(8,128)}, ...) custom-call(bf16[1024,2048]{1,0:T(8,128)(2,1)} %bitcast.7, ...), custom_call_target="tpu_custom_call" | custom-call | tf_op jit(solution)/shard_map/backward/pallas_call | solution.py:1684
  478.7 8.6 %settle.1 = (f32[2816,128]{1,0:T(8,128)}, f32[1024,128]{1,0:T(8,128)}, f32[128,2816]{1,0:T(8,128)}, f32[128,2816]{1,0:T(8,128)}, f32[128,1024]{1,0:T(8,128)}, /*...) custom-call(f32[128,2816]{1,0:T(8,128)} %get-tuple-element.67.refs_0, ...), custom_call_target="tpu_custom_call" | custom-call | tf_op jit(solution)/shard_map/settle/pallas_call | solution.py:1919

commit v7 on v6

--- a/solution.py
+++ b/solution.py
@@ -73,6 +73,8 @@
 
 
 def by_rows(count, body, block=16):
+    block = 2 * block if count % (2 * block) == 0 else block
+
     def step(i, carry):
         body(pl.ds(pl.multiple_of(i * block, block), block))
         return carry

time: 488 us -> 483 us (0.990)
  Pallas kernels: 487 us -> 481 us
    pallas_call x2, Pallas kernels: 478 us -> 472 us  [call(): pl.pallas_call(kernel, out_shape=[jax.ShapeDtypeStruct(shape, dtype) for...]
where the time goes in v7:
time: 483 us; the launch traced here: 482 us
  Pallas kernels  481 us (100%)
    pallas_call x2, Pallas kernels, call(): pl.pallas_call(kernel, out_shape=[jax.ShapeDtypeStruct(shape, dtype) for...  472 us

profile of v7, /device:TPU:0, one launch (start us, length us, event | category | flops | bytes accessed | tf_op | source)
XLA Modules:
  0.0 481.8 jit_solution(8929135426669924645)
XLA Ops:
  0.6 237.3 %forward.1 = (bf16[2048,640]{1,0:T(8,128)(2,1)}, bf16[2048,512]{1,0:T(8,128)(2,1)}, f32[128,128]{1,0:T(8,128)}, bf16[2,512,2048]{2,1,0:T(8,128)(2,1)}, bf16[2,51...) custom-call(bf16[128,1024]{1,0:T(8,128)(2,1)} %refs_0_.1, ...), custom_call_target="tpu_custom_call" | custom-call | tf_op jit(solution)/shard_map/forward/pallas_call | solution.py:1686
  238.0 235.0 %backward.1 = (f32[128,2816]{1,0:T(8,128)}, f32[128,2816]{1,0:T(8,128)}, f32[128,2816]{1,0:T(8,128)}, f32[128,1024]{1,0:T(8,128)}, f32[128,1024]{1,0:T(8,128)}, ...) custom-call(bf16[1024,2048]{1,0:T(8,128)(2,1)} %bitcast.7, ...), custom_call_target="tpu_custom_call" | custom-call | tf_op jit(solution)/shard_map/backward/pallas_call | solution.py:1686
  472.9 8.6 %settle.1 = (f32[2816,128]{1,0:T(8,128)}, f32[1024,128]{1,0:T(8,128)}, f32[128,2816]{1,0:T(8,128)}, f32[128,2816]{1,0:T(8,128)}, f32[128,1024]{1,0:T(8,128)}, /*...) custom-call(f32[128,2816]{1,0:T(8,128)} %get-tuple-element.67.refs_0, ...), custom_call_target="tpu_custom_call" | custom-call | tf_op jit(solution)/shard_map/settle/pallas_call | solution.py:1921
